TPU v7x, 256 devices: a whole 4x4x8 slice. The times are simulated.
256 devices in a mesh: tm: 16 (over z, x_lo), lon: 4 (over x_hi, core), lat: 4 (over y).
Axes of the slice: x: 4 (x_hi: 2, x_lo: 2; x = x_hi * 2 + x_lo), y: 4, z: 8, core: 2. Of those that a mesh axis runs over, the one named last changes fastest.
Arguments:
- iterate: float32 [16, 64, 64, 512], P('tm', None, 'lat', 'lon'), may hold values from -6 to 6
- heating: float32 [16, 64, 64, 512], P('tm', None, 'lat', 'lon'), may hold values from -6 to 6
- initial: float32 [64, 64, 512], P(None, 'lat', 'lon'), may hold values from -6 to 6
- region: int32 [64, 64, 512], P(None, 'lat', 'lon'), may hold values from 0 to 7
- cond_table: float32 [8], replicated, may hold values from 0.3 to 3
Outputs:
- updated: float32 [16, 64, 64, 512], P('tm', None, 'lat', 'lon')
Inputs may be any that keep to these rules, and one draw needn't show every extreme that they name: `region`: class index of each cell.
All inputs are finite; a program needn't handle non-finite values.
Results may differ from a plain program's by a relative error of at most 0.0003.
Values sent between devices are 32-bit elements; how exact they have to be, the bound alone decides.
A program may use at most 128 MiB of HBM per device.

v0:
```python
import jax
import jax.numpy as jnp
from jax import lax
from jax.sharding import PartitionSpec as P

SWEEPS = 4


corner_weight = 0.1


def padded(value, sides, width, wrap):
    for axis, dim in sides:
        peers, length = (lax.axis_size(axis), value.shape[dim])
        up = [(i, (i + 1) % peers) for i in range(peers if wrap else peers - 1)]
        down = [(j, i) for i, j in up]
        last = lax.slice_in_dim(value, length - width, length, axis=dim)
        initial = lax.slice_in_dim(value, 0, width, axis=dim)
        before = lax.ppermute(last, axis, up)
        after = lax.ppermute(initial, axis, down)
        value = jnp.concatenate([before, value, after], axis=dim)
    return value


def passed_along(block, axis, distance):
    devices = range(lax.axis_size(axis))
    route = [(i - distance, i) for i in devices if i - distance in devices]
    return lax.ppermute(block, axis, route)


def harmonic(first, second):
    return 2.0 * first * second / (first + second)


def conductivity(region, cond_table):
    classes = jnp.arange(cond_table.shape[0], dtype=jnp.int32)
    onehot = (region[..., None] == classes).astype(jnp.float32)
    return jnp.sum(onehot * cond_table, axis=-1)


def extend(stack):
    lat_ext = padded(stack, (("lat", 2),), 1, False)
    both = padded(lat_ext, (("lon", 3),), 1, True)
    return jnp.pad(both, ((0, 0), (1, 1), (0, 0), (0, 0)))


def face_weights(kext):
    centre = kext[1:-1, 1:-1, 1:-1]
    return (
        harmonic(centre, kext[:-2, 1:-1, 1:-1]),
        harmonic(centre, kext[2:, 1:-1, 1:-1]),
        harmonic(centre, kext[1:-1, :-2, 1:-1]),
        harmonic(centre, kext[1:-1, 2:, 1:-1]),
        harmonic(centre, kext[1:-1, 1:-1, :-2]),
        harmonic(centre, kext[1:-1, 1:-1, 2:]),
    )


def neighbours(weights, ext):
    near = weights[0] * ext[..., :-2, 1:-1, 1:-1] + weights[1] * ext[..., 2:, 1:-1, 1:-1]
    near = near + weights[2] * ext[..., 1:-1, :-2, 1:-1] + weights[3] * ext[..., 1:-1, 2:, 1:-1]
    near = near + weights[4] * ext[..., 1:-1, 1:-1, :-2] + weights[5] * ext[..., 1:-1, 1:-1, 2:]
    return near


def on_device(iterate, heating, initial, region, cond_table):
    steps = lax.axis_size("tm")
    own = lax.axis_index("tm")
    high = lax.Precision.HIGHEST
    kfield = conductivity(region, cond_table)
    ext = extend(jnp.stack([kfield, iterate[0]]))
    weights = face_weights(ext[0])
    total = weights[0] + weights[1] + weights[2] + weights[3] + weights[4] + weights[5]
    shifted = passed_along(iterate, "tm", 1)[0]
    previous = jnp.where(own == 0, initial, shifted)
    residual = heating[0] + previous - ((1.0 + total) * iterate[0] - neighbours(weights, ext[1]))
    scale_own = corner_weight ** (own.astype(jnp.float32) / steps)
    scaled = residual * scale_own
    zeros = jnp.zeros_like(residual)
    piece = lax.all_gather(scaled[None], "tm", axis=0, tiled=True)
    order = jnp.arange(piece.shape[0], dtype=jnp.int32)
    angle = 2.0 * jnp.pi / steps * (own * order % steps).astype(jnp.float32)
    real_part = jnp.einsum("n,nabc->abc", jnp.cos(angle), piece, precision=high)
    imag_part = (zeros, zeros)[1] - jnp.einsum("n,nabc->abc", jnp.sin(angle), piece, precision=high)
    beta = corner_weight ** (1.0 / steps)
    freq_angle = 2.0 * jnp.pi / steps * (own % steps).astype(jnp.float32)
    diag_re = 1.0 - beta * jnp.cos(freq_angle) + total
    diag_im = beta * jnp.sin(freq_angle) + zeros
    denom = diag_re * diag_re + diag_im * diag_im
    inv_re = diag_re / denom
    inv_im = -diag_im / denom
    sol_re = real_part * inv_re - imag_part * inv_im
    sol_im = real_part * inv_im + imag_part * inv_re
    for sweep in range(SWEEPS - 1):
        near = neighbours(weights, extend(jnp.stack([sol_re, sol_im])))
        rhs_re = real_part + near[0]
        rhs_im = imag_part + near[1]
        sol_re = rhs_re * inv_re - rhs_im * inv_im
        sol_im = rhs_re * inv_im + rhs_im * inv_re
    pieces = (
        lax.all_gather(sol_re[None], "tm", axis=0, tiled=True),
        lax.all_gather(sol_im[None], "tm", axis=0, tiled=True),
    )
    order = jnp.arange(pieces[0].shape[0], dtype=jnp.int32)
    angle = 2.0 * jnp.pi / steps * (order * own % steps).astype(jnp.float32)
    summed = jnp.einsum("k,kabc->abc", jnp.cos(angle), pieces[0], precision=high) - jnp.einsum(
        "k,kabc->abc", jnp.sin(angle), pieces[1], precision=high
    )
    back = summed / steps
    return iterate + (back / scale_own)[None]


def solution(mesh):
    return jax.shard_map(
        on_device,
        mesh=mesh,
        in_specs=(
            P("tm", None, "lat", "lon"),
            P("tm", None, "lat", "lon"),
            P(None, "lat", "lon"),
            P(None, "lat", "lon"),
            P(),
        ),
        out_specs=P("tm", None, "lat", "lon"),
        check_vma=False,
    )
```

profile of v0, /device:TPU:1, one launch (start us, length us, event | category | flops | bytes accessed | tf_op | source)
XLA Modules:
  0.0 730.6 jit_solution(5126643289084944055)
XLA Ops:
  6.5 2.5 select_reduce_fusion
  10.2 4.0 collective-permute-start.1
  15.5 3.7 collective-permute-done.2
  22.2 1.8 copy.57
  24.0 4.8 collective-permute-start.3
  29.3 3.0 collective-permute-start
  35.7 4.0 select_maximum_fusion.15
  41.3 3.9 fusion.45
  45.6 192.4 %all-gather.7.cloned.1.call-done = f32[1024,16,128]{2,1,0:T(8,128)} async-done(((f32[64,16,128]{2,1,0:T(8,128)}), f32[1024,16,128]{2,1,0:T(8,128)}) %all-gather.7.cloned.1.call-update) | async-done | bytes 8388624 | tf_op jit(solution)/shard_map/all_gather | solution.py:80
  238.0 12.6 %fusion.4 = f32[1,64,16,128]{3,0,2,1:T(1,128)S(1)} fusion(f32[16,64,16,128]{3,2,1,0:T(8,128)} %bitcast.108, s32[]{:T(128)S(6)} %axis_index.15), kind=kOutput, calls=%fused_computation.4 | convolution fusion | flops 25166048 | bytes 8912900 | tf_op jit(solution)/shard_map/n,nabc->abc/dot_general | solution.py:84
  250.6 7.8 %fusion.6 = f32[1,64,16,128]{3,0,2,1:T(1,128)S(1)} fusion(f32[16,64,16,128]{3,2,1,0:T(8,128)S(1)} %bitcast.109, s32[]{:T(128)S(6)} %axis_index.15), kind=kOutput, calls=%fused_computation.6 | convolution fusion | flops 25166048 | bytes 8912900 | tf_op jit(solution)/shard_map/n,nabc->abc/dot_general | solution.py:83
  259.1 2.8 collective-permute-start.5
  263.2 3.7 collective-permute-done.6
  270.6 5.2 collective-permute-start.7
  277.3 3.7 collective-permute-done.8
  282.8 4.3 select_maximum_fusion.10
  287.2 2.4 fusion.28
  290.0 3.1 collective-permute-start.9
  294.4 3.7 collective-permute-done.10
  300.0 1.8 copy.67
  305.1 3.7 collective-permute-done.12
  310.6 4.3 select_maximum_fusion.5
  315.0 2.4 fusion.19
  317.8 3.2 collective-permute-start.13
  322.3 3.7 collective-permute-done.14
  332.8 3.7 collective-permute-done.16
  338.3 4.3 select_maximum_fusion
  342.7 2.4 fusion.10
  347.1 177.9 %all-gather.11.cloned.1.call-done = f32[1024,16,128]{2,1,0:T(8,128)} async-done(((f32[64,16,128]{2,1,0:T(8,128)}), f32[1024,16,128]{2,1,0:T(8,128)}) %all-gather.11.cloned.1.call-update) | async-done | bytes 8388624 | tf_op jit(solution)/shard_map/all_gather | solution.py:102
  525.0 12.4 %fusion = f32[1,64,16,128]{3,0,2,1:T(1,128)S(1)} fusion(f32[16,64,16,128]{3,2,1,0:T(8,128)} %bitcast.120, s32[]{:T(128)S(6)} %axis_index.15), kind=kOutput, calls=%fused_computation | convolution fusion | flops 25166048 | bytes 8912900 | tf_op jit(solution)/shard_map/k,kabc->abc/dot_general | solution.py:106
  537.5 173.0 %all-gather.9.cloned.1.call-done = f32[1024,16,128]{2,1,0:T(8,128)} async-done(((f32[64,16,128]{2,1,0:T(8,128)}), f32[1024,16,128]{2,1,0:T(8,128)}) %all-gather.9.cloned.1.call-update) | async-done | bytes 8388624 | tf_op jit(solution)/shard_map/all_gather | solution.py:101
  710.5 12.5 %fusion.2 = f32[1,64,16,128]{3,0,2,1:T(1,128)S(1)} fusion(f32[16,64,16,128]{3,2,1,0:T(8,128)} %bitcast.121, s32[]{:T(128)S(6)} %axis_index.15), kind=kOutput, calls=%fused_computation.2 | convolution fusion | flops 25166048 | bytes 8912900 | tf_op jit(solution)/shard_map/k,kabc->abc/dot_general | solution.py:106
  (147 shorter events, 41.3 us)
Async XLA Ops:
  6.5 231.4 %all-gather.7.cloned.1.call-start = ((), (), s32[]{:S(2)}) async-start(), calls=%async_computation | async-start | bytes 8912896 | tf_op jit(solution)/shard_map/all_gather | solution.py:80
  10.2 5.4 collective-permute-start.1
  14.2 5.0 collective-permute-start.2
  20.5 8.8 %copy-start.4 = (f32[1,64,16,128]{3,2,1,0:T(8,128)S(1)}, f32[1,64,16,128]{3,2,1,0:T(8,128)}, u32[]{:S(2)}) copy-start(f32[1,64,16,128]{3,2,1,0:T(8,128)} %param.5) | copy-start | bytes 1572868
  24.0 8.4 %collective-permute-start.3 = (f32[2,64,18,1]{1,0,3,2:T(2,128)S(1)}, f32[2,64,18,1]{1,0,3,2:T(2,128)S(1)}, u32[]{:S(2)}, u32[]{:S(2)}) collective-permute-start(f32[2,64,18,1]{1,0,3,2:T(2,128)S(1)} %copy.57), channel_id=1, source_target_pairs={{0,4},{4,8},{8,12},{12,0},{1,5},{5,9},{9,13},{13,1},{2,6},{6,10},{... | collective-permute-start | bytes 27656 | tf_op jit(solution)/shard_map/ppermute | solution.py:19
  29.2 4.7 collective-permute-start.4
  29.3 11.9 %collective-permute-start = (f32[1,64,16,128]{3,2,1,0:T(8,128)S(1)}, f32[1,64,16,128]{3,2,1,0:T(8,128)}, u32[]{:S(2)}, u32[]{:S(2)}) collective-permute-start(f32[1,64,16,128]{3,2,1,0:T(8,128)S(1)} %copy-done.4), channel_id=1, source_target_pairs={{0,16},{16,32},{32,48},{48,64},{64,80},{80,96},{96,112},{112,128},... | collective-permute-start | bytes 1572872 | tf_op jit(solution)/shard_map/ppermute | solution.py:28
  45.1 213.3 %copy-start.18 = (f32[64,16,128]{2,1,0:T(8,128)}, f32[64,16,128]{2,1,0:T(8,128)S(1)}, u32[]{:S(2)}) copy-start(f32[64,16,128]{2,1,0:T(8,128)S(1)} %get-tuple-element.8) | copy-start | bytes 1572868
  45.1 213.3 %copy-start.22 = (f32[64,16,128]{2,1,0:T(8,128)}, f32[64,16,128]{2,1,0:T(8,128)S(1)}, u32[]{:S(2)}) copy-start(f32[64,16,128]{2,1,0:T(8,128)S(1)} %get-tuple-element.9) | copy-start | bytes 1572868
  45.1 213.3 %copy-start.26 = (f32[64,16,128]{2,1,0:T(8,128)}, f32[64,16,128]{2,1,0:T(8,128)S(1)}, u32[]{:S(2)}) copy-start(f32[64,16,128]{2,1,0:T(8,128)S(1)} %get-tuple-element.10) | copy-start | bytes 1572868
  45.2 479.8 %all-gather.11.cloned.1.call-start = ((), (), s32[]{:S(2)}) async-start(), calls=%async_computation.2 | async-start | bytes 8912896 | tf_op jit(solution)/shard_map/all_gather | solution.py:102
  238.0 12.6 %copy-start = (f32[1024,16,128]{2,1,0:T(8,128)S(1)}, f32[1024,16,128]{2,1,0:T(8,128)}, u32[]{:S(2)}) copy-start(f32[1024,16,128]{2,1,0:T(8,128)} %all-gather.7.cloned.1.call-done) | copy-start | bytes 25165828
  258.8 8.1 %copy-start.10 = (f32[1,64,16,128]{3,2,1,0:T(8,128)}, f32[1,64,16,128]{3,2,1,0:T(8,128)S(1)}, u32[]{:S(2)}) copy-start(f32[1,64,16,128]{3,2,1,0:T(8,128)S(1)} %get-tuple-element.5) | copy-start | bytes 1572868
  259.0 7.9 %copy-start.16 = (f32[1,64,16,128]{3,2,1,0:T(8,128)}, f32[1,64,16,128]{3,2,1,0:T(8,128)S(1)}, u32[]{:S(2)}) copy-start(f32[1,64,16,128]{3,2,1,0:T(8,128)S(1)} %add_bitcast_fusion.2) | copy-start | bytes 1572868
  259.1 4.1 collective-permute-start.5
  261.9 5.0 collective-permute-start.6
  270.6 6.0 collective-permute-start.7
  276.3 4.7 collective-permute-start.8
  289.8 8.3 %copy-start.12 = (f32[1,64,16,128]{3,2,1,0:T(8,128)}, f32[1,64,16,128]{3,2,1,0:T(8,128)S(1)}, u32[]{:S(2)}) copy-start(f32[1,64,16,128]{3,2,1,0:T(8,128)S(1)} %get-tuple-element.20) | copy-start | bytes 1572868
  289.8 8.2 %copy-start.14 = (f32[1,64,16,128]{3,2,1,0:T(8,128)}, f32[1,64,16,128]{3,2,1,0:T(8,128)S(1)}, u32[]{:S(2)}) copy-start(f32[1,64,16,128]{3,2,1,0:T(8,128)S(1)} %get-tuple-element.21) | copy-start | bytes 1572868
  290.0 4.4 collective-permute-start.9
  293.1 5.0 collective-permute-start.10
  301.8 2.7 collective-permute-start.11
  304.1 4.7 collective-permute-start.12
  317.6 8.4 %copy-start.6 = (f32[1,64,16,128]{3,2,1,0:T(8,128)}, f32[1,64,16,128]{3,2,1,0:T(8,128)S(1)}, u32[]{:S(2)}) copy-start(f32[1,64,16,128]{3,2,1,0:T(8,128)S(1)} %get-tuple-element.18) | copy-start | bytes 1572868
  317.7 8.4 %copy-start.8 = (f32[1,64,16,128]{3,2,1,0:T(8,128)}, f32[1,64,16,128]{3,2,1,0:T(8,128)S(1)}, u32[]{:S(2)}) copy-start(f32[1,64,16,128]{3,2,1,0:T(8,128)S(1)} %get-tuple-element.19) | copy-start | bytes 1572868
  317.8 4.5 collective-permute-start.13
  321.0 5.0 collective-permute-start.14
  329.8 2.5 collective-permute-start.15
  331.8 4.7 collective-permute-start.16
  346.4 364.1 %all-gather.9.cloned.1.call-start = ((), (), s32[]{:S(2)}) async-start(), calls=%async_computation.1 | async-start | bytes 8912896 | tf_op jit(solution)/shard_map/all_gather | solution.py:101
  710.5 12.5 %copy-start.5 = (f32[1,64,16,128]{3,2,1,0:T(8,128)S(1)}, f32[1,64,16,128]{3,2,1,0:T(8,128)}, u32[]{:S(2)}) copy-start(f32[1,64,16,128]{3,2,1,0:T(8,128)} %param.5) | copy-start | bytes 1572868
  (32 other events, 145.7 us)
Sparse Core Ops, SparseCore 0:
  45.3 192.6 all-gather.6
  346.5 178.4 all-gather.10
  526.8 183.6 all-gather.8
where the time goes:
time: 738 us; the launch traced here: 731 us
  waiting for transfers between devices  573 us (78%)
  matrix products  45.4 us (6%)
  other arithmetic  37.1 us (5%)
  starting transfers between devices  35.4 us (5%)
  local copies, waits for them, and re-layouts  25.3 us (3%)
  between operations  14.3 us (2%)
    all_gather x1, waiting for transfers between devices, on_device(): piece = lax.all_gather(scaled[None], 'tm', axis=0, tiled=True)  192 us
    all_gather x1, waiting for transfers between devices, on_device(): lax.all_gather(sol_im[None], 'tm', axis=0, tiled=True)  178 us
    all_gather x1, waiting for transfers between devices, on_device(): lax.all_gather(sol_re[None], 'tm', axis=0, tiled=True)  173 us
    ppermute x8, waiting for transfers between devices, padded(): after = lax.ppermute(initial, axis, down)  27 us
    ppermute x8, starting transfers between devices, padded(): before = lax.ppermute(last, axis, up)  26.5 us
    concatenate x8, other arithmetic, padded(): value = jnp.concatenate([before, value, after], axis=dim)  19 us
  transfers between devices with their start and end apart: 20, of which 15 were waited for; matrix products, arithmetic and copies ran while one was open for 3% of the time, Pallas kernels for 0%

commit v1 on v0

v1 whole, which is shorter than its diff:
```python
import functools
import math

import jax
import jax.numpy as jnp
from jax import lax
from jax.experimental import pallas as pl
from jax.experimental.pallas import tpu as pltpu
from jax.sharding import PartitionSpec as P

MESH = pl.DeviceIdType.MESH
F32 = jnp.float32
CORNER = 0.1
SWEEPS = 3
LP = 8
AP = 8
NA = 16
NX = 128


def harmonic(first, second):
    return 2.0 * first * second / (first + second)


def weighted(pairs):
    total = None
    for coefficient, value in pairs:
        if abs(coefficient) < 1e-12:
            continue
        if abs(coefficient - 1.0) < 1e-12:
            term = value
        elif abs(coefficient + 1.0) < 1e-12:
            total = -value if total is None else total - value
            continue
        else:
            term = value * coefficient
        total = term if total is None else total + term
    return total


def cosine_sums(e, n):
    half, quarter = n // 2, n // 4
    even = [e[m] + e[half - m] for m in range(quarter)]
    odd = [e[m] - e[half - m] for m in range(quarter)]
    out = []
    for k in range(half + 1):
        parts = even if k % 2 == 0 else odd
        pairs = [(math.cos(2 * math.pi * k * m / n), parts[m]) for m in range(quarter)]
        pairs.append((math.cos(2 * math.pi * k * quarter / n), e[quarter]))
        out.append(weighted(pairs))
    return out


def sine_sums(o, n):
    half, quarter = n // 2, n // 4
    plus = [o[m - 1] + o[half - m - 1] for m in range(1, quarter)]
    minus = [o[m - 1] - o[half - m - 1] for m in range(1, quarter)]
    out = []
    for k in range(1, half):
        parts = plus if k % 2 == 1 else minus
        pairs = [(math.sin(2 * math.pi * k * m / n), parts[m - 1]) for m in range(1, quarter)]
        pairs.append((math.sin(2 * math.pi * k * quarter / n), o[quarter - 1]))
        total = weighted(pairs)
        out.append(total if total is not None else jnp.zeros_like(o[0]))
    return out


def pick(index, values):
    chosen = jnp.float32(values[0])
    for i, value in enumerate(values):
        if i > 0:
            chosen = jnp.where(index == i, jnp.float32(value), chosen)
    return chosen


def kernel(
    steps, nlat, nlon,
    u_ref, h_ref, reg_ref, table_ref, init_ref, out_ref,
    kap, wts, pbuf, lat_out, lat_in, lon_out, lon_in,
    rs, rr, spec, coef, xe, xf, edge_out, edge_in, ws, wb,
    init_sem, shift_s, shift_r, side_s, side_r, fwd_s, fwd_r, halo_s, halo_r, back_s, back_r,
):
    levels = u_ref.shape[0] // NA
    zs = steps // 2
    half = steps // 2
    me = lax.axis_index("tm")
    lat = lax.axis_index("lat")
    lon = lax.axis_index("lon")
    z = lax.div(me, 2)
    xl = lax.rem(me, 2)
    q = lax.rem(xl + lat, 2)
    left = lax.rem(lon + nlon - 1, nlon)
    right = lax.rem(lon + 1, nlon)
    sub = lax.broadcasted_iota(jnp.int32, (8, NX), 0)
    lane = lax.broadcasted_iota(jnp.int32, (8, NX), 1)
    zero = jnp.zeros((8, NX), F32)

    def remote(src, dst, send, recv, device):
        return pltpu.make_async_remote_copy(
            src_ref=src, dst_ref=dst, send_sem=send, recv_sem=recv, device_id=device, device_id_type=MESH
        )

    sides = (
        (lat > 0, {"lat": lat - 1}),
        (lat < nlat - 1, {"lat": lat + 1}),
        (None, {"lon": left}),
        (None, {"lon": right}),
    )
    x_low = xl * (1 - q) + (1 - xl) * q
    x_high = xl * q + (1 - xl) * (1 - q)
    homes = (
        (z > 0, {"tm": me - 2}),
        (z < zs - 1, {"tm": me + 2}),
        (q + lat > 0, {"tm": z * 2 + x_low, "lat": lat - (1 - q)}),
        ((1 - q) + (nlat - 1 - lat) > 0, {"tm": z * 2 + x_high, "lat": lat + q}),
        (None, {"lon": left}),
        (None, {"lon": right}),
    )

    def guarded(condition, act):
        if condition is None:
            act()
        else:
            pl.when(condition)(act)

    barrier = pltpu.get_barrier_semaphore()
    for d in range(1, steps):
        pl.semaphore_signal(barrier, inc=1, device_id={"tm": lax.rem(me + d, steps)}, device_id_type=MESH)
    for condition, device in sides:
        guarded(
            condition,
            functools.partial(pl.semaphore_signal, barrier, inc=1, device_id=device, device_id_type=MESH),
        )
    first = pltpu.make_async_copy(init_ref, pbuf, init_sem)

    @pl.when(me == 0)
    def _():
        first.start()

    lat_count = jnp.where(lat > 0, 1, 0) + jnp.where(lat < nlat - 1, 1, 0)
    pl.semaphore_wait(barrier, steps - 1 + 2 + lat_count)

    rows = LP * NA

    def order(i, at):
        odd = lax.rem(i, 2)
        away = zs // 2 + (1 - odd) * lax.div(i, 2) - odd * lax.div(i + 1, 2)
        return lax.rem(at + away, zs)

    def shift_copy(i, at, to):
        part = pl.ds(pl.multiple_of(order(i, at) * rows, 8), rows)
        return remote(u_ref.at[part, :], pbuf.at[part, :], shift_s.at[i], shift_r.at[i], {"tm": to})

    later = lax.rem(me + 1, steps)
    later_z = lax.div(later, 2)

    @pl.when(me < steps - 1)
    def _():
        for i in range(zs):
            shift_copy(i, later_z, later).start()

    kap[pl.ds(0, NA), :] = jnp.zeros((NA, NX), F32)
    kap[pl.ds((levels + 1) * NA, NA), :] = jnp.zeros((NA, NX), F32)
    table = [table_ref[c] for c in range(8)]

    def conduct(g, packs):
        gathered = [zero] * 4
        for j in range(16):
            at = pl.multiple_of(g * 128, 8) + j * 8
            reg = reg_ref[pl.ds(at, 8), :]
            k = jnp.full((8, NX), table[0], F32)
            for c in range(1, 8):
                k = jnp.where(reg == c, table[c], k)
            kap[pl.ds(at + NA, 8), :] = k
            u = u_ref[pl.ds(at, 8), :]
            for f, tile in ((0, u), (1, k)):
                here = lane == j
                low = pltpu.roll(tile, j, 1) if j > 0 else tile
                gathered[f] = jnp.where(here, low, gathered[f])
                gathered[2 + f] = jnp.where(here, pltpu.roll(tile, j + 1, 1), gathered[2 + f])
        mask = lax.div(lane, 16) == g
        return tuple(
            jnp.where(mask, pltpu.roll(gathered[f], g * 16, 1), packs[f]) for f in range(4)
        )

    packs = lax.fori_loop(0, levels // 8, conduct, (zero,) * 4)
    for side in range(2):
        for f in range(2):
            lon_out[side, pl.ds(f * 8, 8), :] = packs[side * 2 + f]
    for g in range(levels // 8):
        for side, row in ((0, 0), (1, NA - 1)):
            lat_out[side, pl.ds(g * 8, 8), :] = u_ref[pl.ds(g * 128 + row, 8, stride=NA), :]
            lat_out[side, pl.ds(levels + g * 8, 8), :] = kap[pl.ds(NA + g * 128 + row, 8, stride=NA), :]

    def side_copy(d):
        if d < 2:
            return remote(lat_out.at[d], lat_in.at[1 - d], side_s.at[d], side_r.at[1 - d], sides[d][1])
        return remote(lon_out.at[d - 2], lon_in.at[3 - d], side_s.at[d], side_r.at[5 - d], sides[d][1])

    def side_arrival(d):
        if d < 2:
            return remote(lat_out.at[d], lat_in.at[d], side_s.at[d], side_r.at[d], sides[d][1])
        return remote(lon_out.at[d - 2], lon_in.at[d - 2], side_s.at[d], side_r.at[d], sides[d][1])

    for d in range(4):
        guarded(sides[d][0], lambda d=d: side_copy(d).start())

    @pl.when(lat == 0)
    def _():
        lat_in[0] = jnp.zeros(lat_in.shape[1:], F32)

    @pl.when(lat == nlat - 1)
    def _():
        lat_in[1] = jnp.zeros(lat_in.shape[1:], F32)

    for b in range(SWEEPS):
        for condition, place in (
            (z == 0, (b, 0, slice(None))),
            (z == zs - 1, (b, LP + 1, slice(None))),
            (q + lat == 0, (b, slice(None), 0)),
            ((1 - q) + (nlat - 1 - lat) == 0, (b, slice(None), AP + 1)),
        ):
            def clear(place=place):
                xe[place] = jnp.zeros((10, 16, NX), F32)

            pl.when(condition)(clear)

    for d in range(4):
        guarded(sides[d][0], lambda d=d: side_arrival(d).wait_recv())

    @pl.when(me == 0)
    def _():
        first.wait()

    gamma = [CORNER ** (n / steps) for n in range(steps)]
    scale = pick(me, gamma)
    u_sides = [lon_in[s, pl.ds(0, 8), :] for s in range(2)]
    k_sides = [lon_in[s, pl.ds(8, 8), :] for s in range(2)]

    def fwd_copy(part, zd, to):
        return remote(
            rs.at[part, pl.ds(pl.multiple_of(zd * 64, 8), 64), :], rr.at[me], fwd_s.at[to], fwd_r.at[me], {"tm": to}
        )

    def chunk(i, carry):
        zd = order(i, z)

        @pl.when(me > 0)
        def _():
            shift_copy(i, z, later).wait_recv()

        def level(l, carry):
            lev = zd * LP + l
            base = pl.multiple_of(lev * NA, 8)
            under = pl.multiple_of(jnp.maximum(lev - 1, 0) * NA, 8)
            over = pl.multiple_of(jnp.minimum(lev + 1, levels - 1) * NA, 8)
            fields = []
            for ref, low, mid, high, off, ends in (
                (u_ref, under, base, over, 0, u_sides),
                (kap, base, base + NA, base + 2 * NA, levels, k_sides),
            ):
                tile = [ref[pl.ds(mid + 8 * t, 8), :] for t in range(2)]
                down = [ref[pl.ds(low + 8 * t, 8), :] for t in range(2)]
                up = [ref[pl.ds(high + 8 * t, 8), :] for t in range(2)]
                row = [
                    jnp.broadcast_to(lat_in[s, pl.ds(off + lev, 1), :], (8, NX)) for s in range(2)
                ]
                one = [pltpu.roll(tile[t], 1, 0) for t in range(2)]
                seven = [pltpu.roll(tile[t], 7, 0) for t in range(2)]
                before = [jnp.where(sub == 0, row[0], one[0]), jnp.where(sub == 0, one[0], one[1])]
                after = [jnp.where(sub == 7, seven[1], seven[0]), jnp.where(sub == 7, row[1], seven[1])]
                west, east = [], []
                for t in range(2):
                    j = lev * 2 + t
                    with_left = jnp.where(lane == NX - 1, pltpu.roll(ends[0], NX - 1 - j, 1), tile[t])
                    west.append(pltpu.roll(with_left, 1, 1))
                    with_right = jnp.where(
                        lane == 0, pltpu.roll(ends[1], lax.rem(NX - j, NX), 1), tile[t]
                    )
                    east.append(pltpu.roll(with_right, NX - 1, 1))
                fields.append((tile, (down, up, before, after, west, east)))
            (u, u_near), (k, k_near) = fields
            for t in range(2):
                at = pl.multiple_of(l * NA, 8) + 8 * t
                total = None
                for f in range(6):
                    w = harmonic(k[t], k_near[f][t])
                    wts[f, pl.ds(at, 8), :] = w
                    term = w * (u_near[f][t] - u[t])
                    total = term if total is None else total + term
                r = (h_ref[pl.ds(base + 8 * t, 8), :] + pbuf[pl.ds(base + 8 * t, 8), :]) - (u[t] - total)
                rs[t, pl.ds(pl.multiple_of(lev * 8, 8), 8), :] = r * scale
            return carry

        def two_levels(m, carry):
            level(m * 2, carry)
            return level(m * 2 + 1, carry)

        lax.fori_loop(0, LP // 2, two_levels, 0)
        for part in range(2):
            to = zd * 2 + lax.rem(part + lat, 2)

            @pl.when(to != me)
            def _():
                fwd_copy(part, zd, to).start()

            @pl.when(to == me)
            def _():
                rr[me] = rs[part, pl.ds(pl.multiple_of(zd * 64, 8), 64), :]

        return carry

    lax.fori_loop(0, zs, chunk, 0)

    beta = CORNER ** (1.0 / steps)
    shift_re = [1.0 - beta * math.cos(2 * math.pi * k / steps) for k in range(half + 1)]
    shift_im = [beta * math.sin(2 * math.pi * k / steps) for k in range(half + 1)]

    def invert(l, carry):
        at = pl.multiple_of(l * NA + q * 8, 8)
        total = wts[0, pl.ds(at, 8), :]
        for f in range(1, 6):
            total = total + wts[f, pl.ds(at, 8), :]
        for k in range(half + 1):
            re = total + shift_re[k]
            if k in (0, half):
                value = 1.0 / re
                row = 0 if k == 0 else 8
                coef[pl.ds(l * 192 + row, 8, stride=24), :] = value
                if k == 0:
                    coef[pl.ds(l * 192 + 16, 8, stride=24), :] = zero
            else:
                share = 1.0 / (re * re + shift_im[k] * shift_im[k])
                real = re * share
                coef[pl.ds(l * 192 + k, 8, stride=24), :] = real
                coef[pl.ds(l * 192 + 8 + k, 8, stride=24), :] = real
                coef[pl.ds(l * 192 + 16 + k, 8, stride=24), :] = share * (-shift_im[k])
        return carry

    lax.fori_loop(0, LP, invert, 0)

    def fwd_arrival(src):
        return remote(rs.at[0, pl.ds(0, 64), :], rr.at[src], fwd_s.at[src], fwd_r.at[src], {"tm": src})

    def await_fwd(d, carry):
        fwd_arrival(lax.rem(me + d, steps)).wait_recv()
        return carry

    lax.fori_loop(1, steps, await_fwd, 0)

    lane64 = lax.rem(lane, 64)

    def pack(l, tiles, packs):
        low, high = zero, zero
        for a in range(AP):
            for f in range(2):
                j = a + 64 * f
                tile = tiles[a][f]
                here = lane == j
                low = jnp.where(here, pltpu.roll(tile, j, 1) if j > 0 else tile, low)
                high = jnp.where(here, pltpu.roll(tile, j + 1, 1), high)
        mask = lax.div(lane64, 8) == l
        return (
            jnp.where(mask, pltpu.roll(low, l * 8, 1), packs[0]),
            jnp.where(mask, pltpu.roll(high, l * 8, 1), packs[1]),
        )

    def divide(l, a, re, im):
        at = pl.multiple_of((l * 8 + a) * 24, 8)
        c_re, c_im, cross = (coef[pl.ds(at + 8 * i, 8), :] for i in range(3))
        return re * c_re - im * cross, im * c_im + re * cross

    def to_spectrum(l, packs):
        at = pl.multiple_of(l * 8, 8)
        r = [rr[n, pl.ds(at, 8), :] for n in range(steps)]
        e = [r[0]] + [r[n] + r[steps - n] for n in range(1, half)] + [r[half]]
        o = [r[n] - r[steps - n] for n in range(1, half)]
        real = cosine_sums(e, steps)
        imag = sine_sums(o, steps)
        for k in range(half):
            spec[pl.ds(l * 128 + k, 8, stride=16), :] = real[k]
        spec[pl.ds(l * 128 + 8, 8, stride=16), :] = real[half]
        for k in range(1, half):
            spec[pl.ds(l * 128 + 8 + k, 8, stride=16), :] = -imag[k - 1]
        tiles = []
        for a in range(AP):
            row = pl.multiple_of((l * 8 + a) * 16, 8)
            x = divide(l, a, spec[pl.ds(row, 8), :], spec[pl.ds(row + 8, 8), :])
            for f in range(2):
                xe[0, l + 1, a + 1, pl.ds(8 * f, 8), :] = x[f]
            tiles.append(x)
        return pack(l, tiles, packs)

    def halo_refs(b, d):
        inner = pl.ds(1, 8)
        if d == 0:
            return xe.at[b, 1, inner], xe.at[b, 0, inner]
        if d == 1:
            return xe.at[b, LP, inner], xe.at[b, LP + 1, inner]
        if d == 2:
            return xe.at[b, inner, 1], xe.at[b, inner, 0]
        if d == 3:
            return xe.at[b, inner, AP], xe.at[b, inner, AP + 1]
        return edge_out.at[b, d - 4], edge_in.at[b, d - 4]

    def halo_copy(b, d):
        other = d + 1 - 2 * (d % 2)
        return remote(
            halo_refs(b, d)[0], halo_refs(b, other)[1], halo_s.at[b, d], halo_r.at[b, other], homes[d][1]
        )

    def halo_arrival(b, d):
        return remote(halo_refs(b, d)[0], halo_refs(b, d)[1], halo_s.at[b, d], halo_r.at[b, d], homes[d][1])

    def exchange(b, packs):
        for s in range(2):
            edge_out[b, s] = packs[s]
        for d in range(6):
            guarded(homes[d][0], lambda d=d: halo_copy(b, d).start())
        for d in range(6):
            guarded(homes[d][0], lambda d=d: halo_arrival(b, d).wait_recv())

    exchange(0, lax.fori_loop(0, LP, to_spectrum, (zero, zero)))

    def sweep(b, last):
        ends = [edge_in[b, s] for s in range(2)]

        def level(l, packs):
            near_ends = [pltpu.roll(ends[s], NX - 8 * l, 1) for s in range(2)]
            tiles = []
            for a in range(AP):
                w = [
                    jnp.broadcast_to(wts[f, pl.ds(l * NA + q * 8 + a, 1), :], (8, NX)) for f in range(6)
                ]
                row = pl.multiple_of((l * 8 + a) * 16, 8)
                rhs = []
                for f in range(2):
                    part = pl.ds(8 * f, 8)
                    j = a + 64 * f
                    x = xe[b, l + 1, a + 1, part, :]
                    with_left = jnp.where(lane == NX - 1, pltpu.roll(near_ends[0], NX - 1 - j, 1), x)
                    with_right = jnp.where(
                        lane == 0, pltpu.roll(near_ends[1], NX - j, 1) if j > 0 else near_ends[1], x
                    )
                    total = spec[pl.ds(row + 8 * f, 8), :]
                    total = total + w[0] * xe[b, l, a + 1, part, :] + w[1] * xe[b, l + 2, a + 1, part, :]
                    total = total + w[2] * xe[b, l + 1, a, part, :] + w[3] * xe[b, l + 1, a + 2, part, :]
                    total = total + w[4] * pltpu.roll(with_left, 1, 1)
                    total = total + w[5] * pltpu.roll(with_right, NX - 1, 1)
                    rhs.append(total)
                x = divide(l, a, rhs[0], rhs[1])
                for f in range(2):
                    if last:
                        xf[pl.ds(row + 8 * f, 8), :] = x[f]
                    else:
                        xe[b + 1, l + 1, a + 1, pl.ds(8 * f, 8), :] = x[f]
                tiles.append(x)
            return packs if last else pack(l, tiles, packs)

        return lax.fori_loop(0, LP, level, (zero, zero))

    for b in range(SWEEPS):
        packs = sweep(b, b == SWEEPS - 1)
        if b < SWEEPS - 1:
            exchange(b + 1, packs)

    def from_spectrum(l, carry):
        x = [xf[pl.ds(l * 128 + k, 8, stride=16), :] for k in range(half)]
        x_half = xf[pl.ds(l * 128 + 8, 8, stride=16), :]
        y = [xf[pl.ds(l * 128 + 8 + k, 8, stride=16), :] for k in range(1, half)]
        even = cosine_sums([x[0] * 0.5] + x[1:] + [x_half * 0.5], steps)
        odd = sine_sums(y, steps)
        at = pl.multiple_of(l * 8, 8)
        ws[0, pl.ds(at, 8), :] = even[0]
        ws[half, pl.ds(at, 8), :] = even[half]
        for n in range(1, half):
            ws[n, pl.ds(at, 8), :] = even[n] - odd[n - 1]
            ws[steps - n, pl.ds(at, 8), :] = even[n] + odd[n - 1]
        return carry

    lax.fori_loop(0, LP, from_spectrum, 0)

    def place(part, zz):
        return wb.at[part, pl.ds(pl.multiple_of(zz * 64, 8), 64), :]

    def back_copy(d):
        to = lax.rem(me + d, steps)
        return remote(ws.at[to], place(q, z), back_s.at[to], back_r.at[me], {"tm": to})

    def start_back(i, carry):
        odd = lax.rem(i, 2)
        d = half + (1 - odd) * lax.div(i, 2) - odd * lax.div(i + 1, 2)
        back_copy(d).start()
        return carry

    lax.fori_loop(0, steps - 1, start_back, 0)
    wb[q, pl.ds(pl.multiple_of(z * 64, 8), 64), :] = ws[me]
    share = pick(me, [2.0 / (steps * g) for g in gamma])

    def finish(i, carry):
        odd = lax.rem(i, 2)
        away = lax.div(i + 1, 2)
        src = lax.rem(me + steps + odd * away - (1 - odd) * away, steps)
        zz = lax.div(src, 2)
        part = lax.rem(lax.rem(src, 2) + lat, 2)

        @pl.when(i > 0)
        def _():
            remote(ws.at[src], place(part, zz), back_s.at[src], back_r.at[src], {"tm": src}).wait_recv()

        for l in range(LP):
            at = pl.multiple_of((zz * LP + l) * NA + part * 8, 8)
            w = wb[part, pl.ds(pl.multiple_of(zz * 64, 8) + l * 8, 8), :]
            out_ref[pl.ds(at, 8), :] = u_ref[pl.ds(at, 8), :] + w * share
        return carry

    lax.fori_loop(0, steps, finish, 0)

    @pl.when(me < steps - 1)
    def _():
        for i in range(zs):
            shift_copy(i, later_z, later).wait_send()

    for d in range(4):
        guarded(sides[d][0], lambda d=d: side_copy(d).wait_send())

    def sent(d, carry):
        to = lax.rem(me + d, steps)
        fwd_copy(0, 0, to).wait_send()
        back_copy(d).wait_send()
        return carry

    lax.fori_loop(1, steps, sent, 0)
    for b in range(SWEEPS):
        for d in range(6):
            guarded(homes[d][0], lambda b=b, d=d: halo_copy(b, d).wait_send())


def on_device(steps, nlat, nlon, iterate, heating, initial, region, cond_table):
    levels = initial.shape[0]
    rows = levels * NA
    zs = steps // 2
    vmem = pl.BlockSpec(memory_space=pltpu.VMEM)
    flat = lambda value: value.reshape(rows, NX)
    dma = pltpu.SemaphoreType.DMA
    out = pl.pallas_call(
        functools.partial(kernel, steps, nlat, nlon),
        out_shape=jax.ShapeDtypeStruct((rows, NX), F32),
        in_specs=[vmem, vmem, vmem, pl.BlockSpec(memory_space=pltpu.SMEM), pl.BlockSpec(memory_space=pl.ANY)],
        out_specs=vmem,
        scratch_shapes=[
            pltpu.VMEM((rows + 2 * NA, NX), F32),
            pltpu.VMEM((6, LP * NA, NX), F32),
            pltpu.VMEM((rows, NX), F32),
            pltpu.VMEM((2, 2 * levels, NX), F32),
            pltpu.VMEM((2, 2 * levels, NX), F32),
            pltpu.VMEM((2, 16, NX), F32),
            pltpu.VMEM((2, 16, NX), F32),
            pltpu.VMEM((2, levels * 8, NX), F32),
            pltpu.VMEM((steps, 64, NX), F32),
            pltpu.VMEM((64 * 16, NX), F32),
            pltpu.VMEM((64 * 24, NX), F32),
            pltpu.VMEM((SWEEPS, LP + 2, AP + 2, 16, NX), F32),
            pltpu.VMEM((64 * 16, NX), F32),
            pltpu.VMEM((SWEEPS, 2, 8, NX), F32),
            pltpu.VMEM((SWEEPS, 2, 8, NX), F32),
            pltpu.VMEM((steps, 64, NX), F32),
            pltpu.VMEM((2, levels * 8, NX), F32),
            dma,
            dma((zs,)),
            dma((zs,)),
            dma((4,)),
            dma((4,)),
            dma((steps,)),
            dma((steps,)),
            dma((SWEEPS, 6)),
            dma((SWEEPS, 6)),
            dma((steps,)),
            dma((steps,)),
        ],
        compiler_params=pltpu.CompilerParams(
            collective_id=0, has_side_effects=True, vmem_limit_bytes=40 * 1024 * 1024
        ),
    )(flat(iterate), flat(heating), flat(region), cond_table, flat(initial))
    return out.reshape(iterate.shape)


def solution(mesh):
    sizes = mesh.shape
    return jax.shard_map(
        functools.partial(on_device, sizes["tm"], sizes["lat"], sizes["lon"]),
        mesh=mesh,
        in_specs=(
            P("tm", None, "lat", "lon"),
            P("tm", None, "lat", "lon"),
            P(None, "lat", "lon"),
            P(None, "lat", "lon"),
            P(),
        ),
        out_specs=P("tm", None, "lat", "lon"),
        check_vma=False,
    )
```

time: 738 us -> 81.7 us (0.11)
  waiting for transfers between devices: 573 us -> 0 us
  Pallas kernels: 0 us -> 75.8 us
  matrix products: 45.4 us -> 0 us
  other arithmetic: 37.1 us -> 0 us
  starting transfers between devices: 35.4 us -> 0 us
  local copies, waits for them, and re-layouts: 25.3 us -> 5.61 us
  between operations: 14.3 us -> 0.01 us
    all_gather x3 -> x0, waiting for transfers between devices: 543 us -> none  [the longest x1 192 us: on_device(): piece = lax.all_gather(scaled[None], 'tm', axis=0, tiled=True)]
    pallas_call x0 -> x1, Pallas kernels: none -> 75.8 us  [on_device(): pl.pallas_call(functools.partial(kernel, steps, nlat, nlon), out_shape=ja...]
    dot_general x4 -> x0, matrix products: 45.4 us -> none  [the longest x1 12.6 us: on_device(): jnp.einsum('n,nabc->abc', jnp.sin(angle), piece, precision=high)]
    ppermute x17 -> x0, starting transfers between devices: 34.9 us -> none  [the longest x8 26.5 us: padded(): before = lax.ppermute(last, axis, up)]
    ppermute x17 -> x0, waiting for transfers between devices: 29.3 us -> none  [the longest x8 27 us: padded(): after = lax.ppermute(initial, axis, down)]
    concatenate x8 -> x0, other arithmetic: 19 us -> none  [padded(): value = jnp.concatenate([before, value, after], axis=dim)]
    slice x12 -> x0, local copies, waits for them, and re-layouts: 15.7 us -> none  [the longest x8 13.9 us: padded(): last = lax.slice_in_dim(value, length - width, length, axis=dim)]
    add x5 -> x0, other arithmetic: 9.31 us -> none  [the longest x3 7.16 us: neighbours(): near + weights[4] * ext[..., 1:-1, 1:-1, :-2]]
  transfers between devices with their start and end apart: 20 -> 0, of which waited for: 15 -> 0; matrix products, arithmetic and copies ran while one was open for 3% -> 0% of each run, Pallas kernels for 0% -> 0%
where the time goes in v1:
time: 81.7 us; the launch traced here: 81.5 us
  Pallas kernels  75.8 us (93%)
  local copies, waits for them, and re-layouts  5.61 us (7%)
    pallas_call x1, Pallas kernels, on_device(): pl.pallas_call(functools.partial(kernel, steps, nlat, nlon), out_shape=ja...  75.8 us
    unnamed x11, local copies, waits for them, and re-layouts  5.61 us

profile of v1, /device:TPU:1, one launch (start us, length us, event | category | flops | bytes accessed | tf_op | source)
XLA Modules:
  0.0 81.5 jit_solution(15800827233144846231)
XLA Ops:
  0.0 0.0 copy-start.4
  0.0 0.7 copy-done.4
  0.7 0.0 copy-start
  0.7 1.0 %copy-done = f32[1,64,16,128]{3,2,1,0:T(8,128)S(1)} copy-done((f32[1,64,16,128]{3,2,1,0:T(8,128)S(1)}, f32[1,64,16,128]{3,2,1,0:T(8,128)}, u32[]{:S(2)}) %copy-start) | copy-done | bytes 524312
  1.7 0.0 copy-start.1
  1.7 1.0 %copy-done.1 = f32[1,64,16,128]{3,2,1,0:T(8,128)S(1)} copy-done((f32[1,64,16,128]{3,2,1,0:T(8,128)S(1)}, f32[1,64,16,128]{3,2,1,0:T(8,128)}, u32[]{:S(2)}) %copy-start.1) | copy-done | bytes 524312
  2.7 0.0 copy-start.2
  2.7 1.0 %copy-done.2 = s32[64,16,128]{2,1,0:T(8,128)S(1)} copy-done((s32[64,16,128]{2,1,0:T(8,128)S(1)}, s32[64,16,128]{2,1,0:T(8,128)}, u32[]{:S(2)}) %copy-start.2) | copy-done | bytes 524312
  3.8 0.0 copy-start.3
  3.8 1.0 %copy-done.3 = f32[64,16,128]{2,1,0:T(8,128)S(1)} copy-done((f32[64,16,128]{2,1,0:T(8,128)S(1)}, f32[64,16,128]{2,1,0:T(8,128)}, u32[]{:S(2)}) %copy-start.3) | copy-done | bytes 524312
  4.8 75.8 %shard_map.55 = f32[1024,128]{1,0:T(8,128)S(1)} custom-call(f32[1024,128]{1,0:T(8,128)S(1)} %bitcast.6, f32[1024,128]{1,0:T(8,128)S(1)} %bitcast.7, s32[1024,128]{1,0:T(8,128)S(1)} %bitcast.8, f32[8]{0:T(128)S(1)} %copy-done.4, f32[1024,128]{1,0:T(8,128)S(1)} %bitcast.9), custom_call_target="tpu_custom_call" | custom-call | tf_op jit(solution)/shard_map/pallas_call | solution.py:546
  80.7 0.8 copy.7
Async XLA Ops:
  0.0 0.7 copy-start.4
  0.7 1.0 %copy-start = (f32[1,64,16,128]{3,2,1,0:T(8,128)S(1)}, f32[1,64,16,128]{3,2,1,0:T(8,128)}, u32[]{:S(2)}) copy-start(f32[1,64,16,128]{3,2,1,0:T(8,128)} %param.5) | copy-start | bytes 1572868
  1.7 1.0 %copy-start.1 = (f32[1,64,16,128]{3,2,1,0:T(8,128)S(1)}, f32[1,64,16,128]{3,2,1,0:T(8,128)}, u32[]{:S(2)}) copy-start(f32[1,64,16,128]{3,2,1,0:T(8,128)} %param.6) | copy-start | bytes 1572868
  2.7 1.0 %copy-start.2 = (s32[64,16,128]{2,1,0:T(8,128)S(1)}, s32[64,16,128]{2,1,0:T(8,128)}, u32[]{:S(2)}) copy-start(s32[64,16,128]{2,1,0:T(8,128)} %param.8) | copy-start | bytes 1572868
  3.8 1.0 %copy-start.3 = (f32[64,16,128]{2,1,0:T(8,128)S(1)}, f32[64,16,128]{2,1,0:T(8,128)}, u32[]{:S(2)}) copy-start(f32[64,16,128]{2,1,0:T(8,128)} %param.7) | copy-start | bytes 1572868

commit v2 on v1

v2 whole, which is shorter than its diff:
```python
import functools
import math

import jax
import jax.numpy as jnp
from jax import lax
from jax.experimental import pallas as pl
from jax.experimental.pallas import tpu as pltpu
from jax.sharding import PartitionSpec as P

MESH = pl.DeviceIdType.MESH
F32 = jnp.float32
CORNER = 0.1
SWEEPS = 3
LP = 8
AP = 8
NA = 16
NX = 128
VMEM_LIMIT = 62 * 1024 * 1024


def harmonic(first, second):
    return 2.0 * first * second / (first + second)


def weighted(pairs):
    total = None
    for coefficient, value in pairs:
        if abs(coefficient) < 1e-12:
            continue
        if abs(coefficient - 1.0) < 1e-12:
            term = value
        elif abs(coefficient + 1.0) < 1e-12:
            total = -value if total is None else total - value
            continue
        else:
            term = value * coefficient
        total = term if total is None else total + term
    return total


def cosine_sums(e, n):
    half, quarter = n // 2, n // 4
    even = [e[m] + e[half - m] for m in range(quarter)]
    odd = [e[m] - e[half - m] for m in range(quarter)]
    out = []
    for k in range(half + 1):
        parts = even if k % 2 == 0 else odd
        pairs = [(math.cos(2 * math.pi * k * m / n), parts[m]) for m in range(quarter)]
        pairs.append((math.cos(2 * math.pi * k * quarter / n), e[quarter]))
        out.append(weighted(pairs))
    return out


def sine_sums(o, n):
    half, quarter = n // 2, n // 4
    plus = [o[m - 1] + o[half - m - 1] for m in range(1, quarter)]
    minus = [o[m - 1] - o[half - m - 1] for m in range(1, quarter)]
    out = []
    for k in range(1, half):
        parts = plus if k % 2 == 1 else minus
        pairs = [(math.sin(2 * math.pi * k * m / n), parts[m - 1]) for m in range(1, quarter)]
        pairs.append((math.sin(2 * math.pi * k * quarter / n), o[quarter - 1]))
        total = weighted(pairs)
        out.append(total if total is not None else jnp.zeros_like(o[0]))
    return out


def pick(index, values):
    chosen = jnp.float32(values[0])
    for i, value in enumerate(values):
        if i > 0:
            chosen = jnp.where(index == i, jnp.float32(value), chosen)
    return chosen


def kernel(
    steps, nlat, nlon,
    u_hbm, u_parts, h_hbm, reg_hbm, init_hbm, table_ref, out_ref,
    u_ref, h_ref, reg_ref, kap, wts, pbuf, lat_out, lat_in, lon_out, lon_in, lon_mix,
    rs, rr, ur, spec, coef, xe, xf, edge_out, edge_in, ws, wb,
    local, shift_s, shift_r, side_s, side_r, state_s, state_r, fwd_s, fwd_r,
    lev_s, lev_r, lat_s, lat_r, lon_s, lon_r, back_s, back_r,
):
    levels = u_ref.shape[0] // NA
    zs = steps // 2
    half = steps // 2
    me = lax.axis_index("tm")
    lat = lax.axis_index("lat")
    lon = lax.axis_index("lon")
    z = lax.div(me, 2)
    xl = lax.rem(me, 2)
    q = lax.rem(xl + lat, 2)
    left = lax.rem(lon + nlon - 1, nlon)
    right = lax.rem(lon + 1, nlon)
    sub = lax.broadcasted_iota(jnp.int32, (8, NX), 0)
    lane = lax.broadcasted_iota(jnp.int32, (8, NX), 1)
    lane_pair = lax.div(lane, 2)
    odd_lane = lax.rem(lane, 2) == 1
    first_lane = lane == 0
    last_lane = lane == NX - 1
    zero = jnp.zeros((8, NX), F32)

    def remote(src, dst, send, recv, device):
        return pltpu.make_async_remote_copy(
            src_ref=src, dst_ref=dst, send_sem=send, recv_sem=recv, device_id=device, device_id_type=MESH
        )

    def guarded(condition, act):
        if condition is None:
            act()
        else:
            pl.when(condition)(act)

    sides = (
        (lat > 0, {"lat": lat - 1}),
        (lat < nlat - 1, {"lat": lat + 1}),
        (None, {"lon": left}),
        (None, {"lon": right}),
    )
    x_low = xl * (1 - q) + (1 - xl) * q
    x_high = xl * q + (1 - xl) * (1 - q)
    lev_sides = ((z > 0, {"tm": me - 2}), (z < zs - 1, {"tm": me + 2}))
    lat_sides = (
        (q + lat > 0, {"tm": z * 2 + x_low, "lat": lat - (1 - q)}),
        ((1 - q) + (nlat - 1 - lat) > 0, {"tm": z * 2 + x_high, "lat": lat + q}),
    )
    lon_sides = ((None, {"lon": left}), (None, {"lon": right}))

    barrier = pltpu.get_barrier_semaphore()
    for d in range(1, steps):
        pl.semaphore_signal(barrier, inc=1, device_id={"tm": lax.rem(me + d, steps)}, device_id_type=MESH)
    for condition, device in sides:
        guarded(
            condition,
            functools.partial(pl.semaphore_signal, barrier, inc=1, device_id=device, device_id_type=MESH),
        )

    take_reg = pltpu.make_async_copy(reg_hbm, reg_ref, local.at[0])
    take_u = pltpu.make_async_copy(u_hbm, u_ref, local.at[1])
    take_h = pltpu.make_async_copy(h_hbm, h_ref, local.at[2])
    take_init = pltpu.make_async_copy(init_hbm, pbuf, local.at[3])
    take_reg.start()
    take_u.start()
    take_h.start()

    @pl.when(me == 0)
    def _():
        take_init.start()

    for b in range(SWEEPS):
        for condition, place in (
            (z == 0, (b, 0, slice(None))),
            (z == zs - 1, (b, 1, slice(None))),
            (q + lat == 0, (b, slice(None), 0)),
            ((1 - q) + (nlat - 1 - lat) == 0, (b, slice(None), AP + 1)),
        ):
            def clear(place=place):
                xe[place] = jnp.zeros((10, 16, NX), F32)

            pl.when(condition)(clear)

    @pl.when(lat == 0)
    def _():
        lat_in[0] = jnp.zeros(lat_in.shape[1:], F32)

    @pl.when(lat == nlat - 1)
    def _():
        lat_in[1] = jnp.zeros(lat_in.shape[1:], F32)

    @pl.when(jnp.logical_and(me > 0, xl == 0))
    def _():
        pbuf[...] = jnp.zeros(pbuf.shape, F32)

    kap[pl.ds(0, NA), :] = jnp.zeros((NA, NX), F32)
    kap[pl.ds((levels + 1) * NA, NA), :] = jnp.zeros((NA, NX), F32)
    table = [table_ref[c] for c in range(8)]
    take_reg.wait()
    take_u.wait()

    for group in range((levels + 31) // 32):
        def conduct(g, packs):
            gathered = [zero, zero]
            for j in range(16):
                at = pl.multiple_of((group * 4 + g) * 128, 8) + j * 8
                reg = reg_ref[pl.ds(at, 8), :]
                k = jnp.full((8, NX), table[0], F32)
                for c in range(1, 8):
                    k = jnp.where(reg == c, table[c], k)
                kap[pl.ds(at + NA, 8), :] = k
                u = u_ref[pl.ds(at, 8), :]
                for f, tile in ((0, u), (1, k)):
                    gathered[f] = jnp.where(lane_pair == j, pltpu.roll(tile, 2 * j + 1, 1), gathered[f])
            mask = lax.div(lane, 32) == g
            return tuple(jnp.where(mask, pltpu.roll(gathered[f], g * 32, 1), packs[f]) for f in range(2))

        packs = lax.fori_loop(0, min(4, levels // 8 - 4 * group), conduct, (zero, zero))
        for f in range(2):
            lon_out[group, f] = packs[f]
    for g in range(levels // 8):
        for side, row in ((0, 0), (1, NA - 1)):
            lat_out[side, pl.ds(g * 8, 8), :] = u_ref[pl.ds(g * 128 + row, 8, stride=NA), :]
            lat_out[side, pl.ds(levels + g * 8, 8), :] = kap[pl.ds(NA + g * 128 + row, 8, stride=NA), :]

    lat_count = jnp.where(lat > 0, 1, 0) + jnp.where(lat < nlat - 1, 1, 0)
    pl.semaphore_wait(barrier, steps - 1 + 2 + lat_count)

    def side_copy(d):
        if d < 2:
            return remote(lat_out.at[d], lat_in.at[1 - d], side_s.at[d], side_r.at[1 - d], sides[d][1])
        return remote(lon_out, lon_in.at[3 - d], side_s.at[d], side_r.at[5 - d], sides[d][1])

    def side_arrival(d):
        if d < 2:
            return remote(lat_out.at[d], lat_in.at[d], side_s.at[d], side_r.at[d], sides[d][1])
        return remote(lon_out, lon_in.at[d - 2], side_s.at[d], side_r.at[d], sides[d][1])

    for d in range(4):
        guarded(sides[d][0], lambda d=d: side_copy(d).start())

    def order(i, at):
        odd = lax.rem(i, 2)
        away = zs // 2 + (1 - odd) * lax.div(i, 2) - odd * lax.div(i + 1, 2)
        return lax.rem(at + away, zs)

    rows = LP * NA

    def shift_copy(i):
        part = pl.ds(pl.multiple_of(order(i, z) * rows, 8), rows)
        return remote(u_hbm.at[part, :], pbuf.at[part, :], shift_s.at[i], shift_r.at[i], {"tm": me + 1 - 2 * xl})

    @pl.when(xl == 0)
    def _():
        for i in range(zs):
            shift_copy(i).start()

    def state_copy(to):
        part = lax.rem(lax.rem(to, 2) + lat, 2)
        return remote(
            u_parts.at[pl.ds(lax.div(to, 2) * LP, LP), part], ur.at[z], state_s.at[to], state_r.at[z], {"tm": to}
        )

    sends_state = jnp.logical_and(xl == 1, z < zs - 1)

    @pl.when(sends_state)
    def _():
        def send(i, carry):
            odd = lax.rem(i, 2)
            d = half + (1 - odd) * lax.div(i, 2) - odd * lax.div(i + 1, 2)
            state_copy(lax.rem(me + d, steps)).start()
            return carry

        lax.fori_loop(0, steps - 1, send, 0)
        for l in range(LP):
            row = pl.multiple_of((z * LP + l) * NA + q * 8, 8)
            ur[z, l] = u_ref[pl.ds(row, 8), :]

    take_h.wait()

    @pl.when(me == 0)
    def _():
        take_init.wait()

    for d in range(4):
        guarded(sides[d][0], lambda d=d: side_arrival(d).wait_recv())
    for group in range((levels + 31) // 32):
        for f in range(2):
            lon_mix[group, f] = jnp.where(odd_lane, lon_in[1, group, f], lon_in[0, group, f])

    gamma = [CORNER ** (n / steps) for n in range(steps)]
    scale = pick(me, gamma)

    def fwd_copy(part, zd, to):
        return remote(
            rs.at[part, pl.ds(pl.multiple_of(zd * 64, 8), 64), :], rr.at[me], fwd_s.at[to], fwd_r.at[me], {"tm": to}
        )

    def chunk(i, carry):
        zd = order(i, z)

        @pl.when(xl == 1)
        def _():
            shift_copy(i).wait_recv()

        def level(l):
            lev = zd * LP + l
            base = pl.multiple_of(lev * NA, 8)
            under = pl.multiple_of(jnp.maximum(lev - 1, 0) * NA, 8)
            over = pl.multiple_of(jnp.minimum(lev + 1, levels - 1) * NA, 8)
            group = lax.div(lev, 32)
            fields = []
            for f, ref, low, mid, high in (
                (0, u_ref, under, base, over),
                (1, kap, base, base + NA, base + 2 * NA),
            ):
                tile = [ref[pl.ds(mid + 8 * t, 8), :] for t in range(2)]
                down = [ref[pl.ds(low + 8 * t, 8), :] for t in range(2)]
                up = [ref[pl.ds(high + 8 * t, 8), :] for t in range(2)]
                row = [
                    jnp.broadcast_to(lat_in[s, pl.ds(f * levels + lev, 1), :], (8, NX)) for s in range(2)
                ]
                one = [pltpu.roll(tile[t], 1, 0) for t in range(2)]
                seven = [pltpu.roll(tile[t], 7, 0) for t in range(2)]
                before = [jnp.where(sub == 0, row[0], one[0]), jnp.where(sub == 0, one[0], one[1])]
                after = [jnp.where(sub == 7, seven[1], seven[0]), jnp.where(sub == 7, row[1], seven[1])]
                ends = lon_mix[group, f]
                west, east = [], []
                for t in range(2):
                    halo = pltpu.roll(ends, NX - 1 - 2 * (lax.rem(lev, 32) * 2 + t), 1)
                    west.append(pltpu.roll(jnp.where(last_lane, halo, tile[t]), 1, 1))
                    east.append(pltpu.roll(jnp.where(first_lane, halo, tile[t]), NX - 1, 1))
                fields.append((tile, (down, up, before, after, west, east)))
            (u, u_near), (k, k_near) = fields
            for t in range(2):
                at = pl.multiple_of(l * NA, 8) + 8 * t
                total = None
                for f in range(6):
                    w = harmonic(k[t], k_near[f][t])
                    wts[f, pl.ds(at, 8), :] = w
                    term = w * (u_near[f][t] - u[t])
                    total = term if total is None else total + term
                r = (h_ref[pl.ds(base + 8 * t, 8), :] + pbuf[pl.ds(base + 8 * t, 8), :]) - (u[t] - total)
                rs[t, pl.ds(pl.multiple_of(lev * 8, 8), 8), :] = r * scale

        def some_levels(m, carry):
            for l in range(4):
                level(m * 4 + l)
            return carry

        lax.fori_loop(0, LP // 4, some_levels, 0)
        for part in range(2):
            to = zd * 2 + lax.rem(part + lat, 2)

            @pl.when(to != me)
            def _():
                fwd_copy(part, zd, to).start()

            @pl.when(to == me)
            def _():
                rr[me] = rs[part, pl.ds(pl.multiple_of(zd * 64, 8), 64), :]

        return carry

    lax.fori_loop(0, zs, chunk, 0)

    beta = CORNER ** (1.0 / steps)
    shift_re = [1.0 - beta * math.cos(2 * math.pi * k / steps) for k in range(half + 1)]
    shift_im = [beta * math.sin(2 * math.pi * k / steps) for k in range(half + 1)]

    def invert(l, carry):
        at = pl.multiple_of(l * NA + q * 8, 8)
        total = wts[0, pl.ds(at, 8), :]
        for f in range(1, 6):
            total = total + wts[f, pl.ds(at, 8), :]
        for k in range(half + 1):
            re = total + shift_re[k]
            if k in (0, half):
                value = 1.0 / re
                row = 0 if k == 0 else 8
                coef[pl.ds(l * 192 + row, 8, stride=24), :] = value
                if k == 0:
                    coef[pl.ds(l * 192 + 16, 8, stride=24), :] = zero
            else:
                share = 1.0 / (re * re + shift_im[k] * shift_im[k])
                real = re * share
                coef[pl.ds(l * 192 + k, 8, stride=24), :] = real
                coef[pl.ds(l * 192 + 8 + k, 8, stride=24), :] = real
                coef[pl.ds(l * 192 + 16 + k, 8, stride=24), :] = share * (-shift_im[k])
        return carry

    lax.fori_loop(0, LP, invert, 0)

    def await_fwd(d, carry):
        src = lax.rem(me + d, steps)
        remote(rs.at[0, pl.ds(0, 64), :], rr.at[src], fwd_s.at[src], fwd_r.at[src], {"tm": src}).wait_recv()
        return carry

    lax.fori_loop(1, steps, await_fwd, 0)
    for i in range(zs - 1):

        @pl.when(me != 2 * i + 1)
        def _():
            remote(u_parts.at[pl.ds(0, LP), 0], ur.at[i], state_s.at[i], state_r.at[i], {"tm": 2 * i + 1}).wait_recv()

    def sent_index(m, s):
        return 2 + 2 * m + s

    def inner_index(m, s):
        return jnp.where(m == LP // 2 - 1, LP + 1 - s, 4 + 2 * m + s)

    def level_of(m, s):
        return m + s * (LP - 1 - 2 * m)

    def divide(l, a, re, im):
        at = pl.multiple_of((l * 8 + a) * 24, 8)
        c_re, c_im, cross = (coef[pl.ds(at + 8 * i, 8), :] for i in range(3))
        return re * c_re - im * cross, im * c_im + re * cross

    class Packed:
        def __init__(self):
            self.parts = [zero, zero]

        def add(self, s, a, f, tile):
            j = (s * AP + a) * 2 + f
            self.parts[f] = jnp.where(lane_pair == j, pltpu.roll(tile, 2 * j + 1, 1), self.parts[f])

        def value(self):
            return jnp.where(lax.rem(lane_pair, 2) == 0, self.parts[0], self.parts[1])

    inner = pl.ds(1, AP)

    def lev_copy(b, d):
        return remote(
            xe.at[b, 2 + d, inner], xe.at[b, 1 - d, inner], lev_s.at[b, d], lev_r.at[b, 1 - d], lev_sides[d][1]
        )

    def lev_arrival(b, d):
        return remote(xe.at[b, 2 + d, inner], xe.at[b, d, inner], lev_s.at[b, d], lev_r.at[b, d], lev_sides[d][1])

    def lat_copy(b, m, d):
        pair = pl.ds(2 + 2 * m, 2)
        return remote(
            xe.at[b, pair, 1 + d * (AP - 1)], xe.at[b, pair, (1 - d) * (AP + 1)],
            lat_s.at[b, m, d], lat_r.at[b, m, 1 - d], lat_sides[d][1],
        )

    def lat_arrival(b, m, d):
        pair = pl.ds(2 + 2 * m, 2)
        return remote(
            xe.at[b, pair, 1 + d * (AP - 1)], xe.at[b, pair, d * (AP + 1)],
            lat_s.at[b, m, d], lat_r.at[b, m, d], lat_sides[d][1],
        )

    def lon_copy(b, m, d):
        return remote(
            edge_out.at[b, m], edge_in.at[b, m, 1 - d], lon_s.at[b, m, d], lon_r.at[b, m, 1 - d], lon_sides[d][1]
        )

    def lon_arrival(b, m, d):
        return remote(edge_out.at[b, m], edge_in.at[b, m, d], lon_s.at[b, m, d], lon_r.at[b, m, d], lon_sides[d][1])

    def send_edges(b, m, packed):
        edge_out[b, m] = packed.value()

        @pl.when(m == 0)
        def _():
            for d in range(2):
                guarded(lev_sides[d][0], lambda d=d: lev_copy(b, d).start())

        for d in range(2):
            lon_copy(b, m, d).start()
        for d in range(2):
            guarded(lat_sides[d][0], lambda d=d: lat_copy(b, m, d).start())

    def await_edges(b, m):
        @pl.when(m == 0)
        def _():
            for d in range(2):
                guarded(lev_sides[d][0], lambda d=d: lev_arrival(b, d).wait_recv())

        for d in range(2):
            guarded(lat_sides[d][0], lambda d=d: lat_arrival(b, m, d).wait_recv())
        for d in range(2):
            lon_arrival(b, m, d).wait_recv()

    def to_spectrum(m, carry):
        packed = Packed()
        for s in range(2):
            l = level_of(m, s)
            at = pl.multiple_of(l * 8, 8)
            r = [rr[n, pl.ds(at, 8), :] for n in range(steps)]
            for n in range(2, steps, 2):
                r[n] = r[n] + ur[n // 2 - 1, l] * gamma[n]
            e = [r[0]] + [r[n] + r[steps - n] for n in range(1, half)] + [r[half]]
            o = [r[n] - r[steps - n] for n in range(1, half)]
            real = cosine_sums(e, steps)
            imag = sine_sums(o, steps)
            for k in range(half):
                spec[pl.ds(l * 128 + k, 8, stride=16), :] = real[k]
            spec[pl.ds(l * 128 + 8, 8, stride=16), :] = real[half]
            for k in range(1, half):
                spec[pl.ds(l * 128 + 8 + k, 8, stride=16), :] = -imag[k - 1]
        for s in range(2):
            l = level_of(m, s)
            for a in range(AP):
                row = pl.multiple_of((l * 8 + a) * 16, 8)
                x = divide(l, a, spec[pl.ds(row, 8), :], spec[pl.ds(row + 8, 8), :])
                for f in range(2):
                    xe[0, sent_index(m, s), a + 1, pl.ds(8 * f, 8), :] = x[f]
                    packed.add(s, a, f, x[f])
        send_edges(0, m, packed)
        return carry

    lax.fori_loop(0, LP // 2, to_spectrum, 0)

    def back_copy(to, first, count):
        part = pl.ds(pl.multiple_of(first, 8), count)
        return remote(ws.at[to, part], wb.at[me, part], back_s.at[to], back_r.at[me], {"tm": to})

    def from_spectrum(m, s):
        base = s * 128
        x = [xf[pl.ds(base + k, 8, stride=16), :] for k in range(half)]
        x_half = xf[pl.ds(base + 8, 8, stride=16), :]
        y = [xf[pl.ds(base + 8 + k, 8, stride=16), :] for k in range(1, half)]
        even = cosine_sums([x[0] * 0.5] + x[1:] + [x_half * 0.5], steps)
        odd = sine_sums(y, steps)
        at = pl.ds(pl.multiple_of(m * 16, 8) + s * 8, 8)
        ws[0, at, :] = even[0]
        ws[half, at, :] = even[half]
        for n in range(1, half):
            ws[n, at, :] = even[n] - odd[n - 1]
            ws[steps - n, at, :] = even[n] + odd[n - 1]

    def sweep(b, last):
        def pair(m, carry):
            await_edges(b, m)
            ends = jnp.where(odd_lane, edge_in[b, m, 1], edge_in[b, m, 0])
            packed = Packed()
            for s in range(2):
                l = level_of(m, s)
                i = sent_index(m, s)
                beyond = (i - 2, inner_index(m, s))
                under, over = beyond if s == 0 else beyond[::-1]
                for a in range(AP):
                    w = [
                        jnp.broadcast_to(wts[f, pl.ds(l * NA + q * 8 + a, 1), :], (8, NX)) for f in range(6)
                    ]
                    row = pl.multiple_of((l * 8 + a) * 16, 8)
                    rhs = []
                    for f in range(2):
                        part = pl.ds(8 * f, 8)
                        j = (s * AP + a) * 2 + f
                        x = xe[b, i, a + 1, part, :]
                        halo = pltpu.roll(ends, NX - 1 - 2 * j, 1)
                        total = spec[pl.ds(row + 8 * f, 8), :]
                        total = total + w[0] * xe[b, under, a + 1, part, :] + w[1] * xe[b, over, a + 1, part, :]
                        total = total + w[2] * xe[b, i, a, part, :] + w[3] * xe[b, i, a + 2, part, :]
                        total = total + w[4] * pltpu.roll(jnp.where(last_lane, halo, x), 1, 1)
                        total = total + w[5] * pltpu.roll(jnp.where(first_lane, halo, x), NX - 1, 1)
                        rhs.append(total)
                    x = divide(l, a, rhs[0], rhs[1])
                    for f in range(2):
                        if last:
                            xf[pl.ds((s * AP + a) * 16 + 8 * f, 8), :] = x[f]
                        else:
                            xe[b + 1, i, a + 1, pl.ds(8 * f, 8), :] = x[f]
                            packed.add(s, a, f, x[f])
            if not last:
                send_edges(b + 1, m, packed)
            else:
                for s in range(2):
                    from_spectrum(m, s)

                @pl.when(lax.rem(m, 2) == 1)
                def _():
                    def send(i, carry):
                        odd = lax.rem(i, 2)
                        d = half + (1 - odd) * lax.div(i, 2) - odd * lax.div(i + 1, 2)
                        back_copy(lax.rem(me + d, steps), (m - 1) * 16, 32).start()
                        return carry

                    lax.fori_loop(0, steps - 1, send, 0)

            return carry

        lax.fori_loop(0, LP // 2, pair, 0)

    for b in range(SWEEPS):
        sweep(b, b == SWEEPS - 1)

    wb[me] = ws[me]
    share = pick(me, [2.0 / (steps * g) for g in gamma])

    def finish(i, carry):
        odd = lax.rem(i, 2)
        away = lax.div(i + 1, 2)
        src = lax.rem(me + steps + odd * away - (1 - odd) * away, steps)
        zz = lax.div(src, 2)
        part = lax.rem(lax.rem(src, 2) + lat, 2)

        @pl.when(i > 0)
        def _():
            remote(ws.at[src], wb.at[src], back_s.at[src], back_r.at[src], {"tm": src}).wait_recv()

        for m in range(LP // 2):
            for s in range(2):
                at = pl.multiple_of((zz * LP + level_of(m, s)) * NA + part * 8, 8)
                out_ref[pl.ds(at, 8), :] = u_ref[pl.ds(at, 8), :] + wb[src, pl.ds(m * 16 + s * 8, 8), :] * share
        return carry

    lax.fori_loop(0, steps, finish, 0)

    @pl.when(xl == 0)
    def _():
        for i in range(zs):
            shift_copy(i).wait_send()

    for d in range(4):
        guarded(sides[d][0], lambda d=d: side_copy(d).wait_send())

    def sent(d, carry):
        to = lax.rem(me + d, steps)
        fwd_copy(0, 0, to).wait_send()
        back_copy(to, 0, 64).wait_send()

        @pl.when(sends_state)
        def _():
            state_copy(to).wait_send()

        return carry

    lax.fori_loop(1, steps, sent, 0)
    for b in range(SWEEPS):
        for d in range(2):
            guarded(lev_sides[d][0], lambda b=b, d=d: lev_copy(b, d).wait_send())

        def edges_sent(m, carry, b=b):
            for d in range(2):
                guarded(lat_sides[d][0], lambda d=d: lat_copy(b, m, d).wait_send())
                lon_copy(b, m, d).wait_send()
            return carry

        lax.fori_loop(0, LP // 2, edges_sent, 0)


def on_device(steps, nlat, nlon, iterate, heating, initial, region, cond_table):
    levels = initial.shape[0]
    rows = levels * NA
    zs = steps // 2
    groups = (levels + 31) // 32
    pairs = LP // 2
    vmem = pl.BlockSpec(memory_space=pltpu.VMEM)
    anywhere = pl.BlockSpec(memory_space=pl.ANY)
    flat = lambda value: value.reshape(rows, NX)
    dma = pltpu.SemaphoreType.DMA
    out = pl.pallas_call(
        functools.partial(kernel, steps, nlat, nlon),
        out_shape=jax.ShapeDtypeStruct((rows, NX), F32),
        in_specs=[anywhere] * 5 + [pl.BlockSpec(memory_space=pltpu.SMEM)],
        out_specs=vmem,
        scratch_shapes=[
            pltpu.VMEM((rows, NX), F32),
            pltpu.VMEM((rows, NX), F32),
            pltpu.VMEM((rows, NX), jnp.int32),
            pltpu.VMEM((rows + 2 * NA, NX), F32),
            pltpu.VMEM((6, LP * NA, NX), F32),
            pltpu.VMEM((rows, NX), F32),
            pltpu.VMEM((2, 2 * levels, NX), F32),
            pltpu.VMEM((2, 2 * levels, NX), F32),
            pltpu.VMEM((groups, 2, 8, NX), F32),
            pltpu.VMEM((2, groups, 2, 8, NX), F32),
            pltpu.VMEM((groups, 2, 8, NX), F32),
            pltpu.VMEM((2, levels * 8, NX), F32),
            pltpu.VMEM((steps, 64, NX), F32),
            pltpu.VMEM((zs, LP, 8, NX), F32),
            pltpu.VMEM((64 * 16, NX), F32),
            pltpu.VMEM((64 * 24, NX), F32),
            pltpu.VMEM((SWEEPS, LP + 2, AP + 2, 16, NX), F32),
            pltpu.VMEM((16 * 16, NX), F32),
            pltpu.VMEM((SWEEPS, pairs, 8, NX), F32),
            pltpu.VMEM((SWEEPS, pairs, 2, 8, NX), F32),
            pltpu.VMEM((steps, 64, NX), F32),
            pltpu.VMEM((steps, 64, NX), F32),
            dma((4,)),
            dma((zs,)),
            dma((zs,)),
            dma((4,)),
            dma((4,)),
            dma((steps,)),
            dma((zs,)),
            dma((steps,)),
            dma((steps,)),
            dma((SWEEPS, 2)),
            dma((SWEEPS, 2)),
            dma((SWEEPS, pairs, 2)),
            dma((SWEEPS, pairs, 2)),
            dma((SWEEPS, pairs, 2)),
            dma((SWEEPS, pairs, 2)),
            dma((steps,)),
            dma((steps,)),
        ],
        compiler_params=pltpu.CompilerParams(
            collective_id=0, has_side_effects=True, vmem_limit_bytes=VMEM_LIMIT
        ),
    )(flat(iterate), iterate.reshape(levels, 2, AP, NX), flat(heating), flat(region), flat(initial), cond_table)
    return out.reshape(iterate.shape)


def solution(mesh):
    sizes = mesh.shape
    return jax.shard_map(
        functools.partial(on_device, sizes["tm"], sizes["lat"], sizes["lon"]),
        mesh=mesh,
        in_specs=(
            P("tm", None, "lat", "lon"),
            P("tm", None, "lat", "lon"),
            P(None, "lat", "lon"),
            P(None, "lat", "lon"),
            P(),
        ),
        out_specs=P("tm", None, "lat", "lon"),
        check_vma=False,
    )
```

time: 81.7 us -> 66.6 us (0.82)
  Pallas kernels: 75.8 us -> 64.6 us
  local copies, waits for them, and re-layouts: 5.61 us -> 1.87 us
    pallas_call x1, Pallas kernels: 75.8 us -> 64.6 us  [on_device(): pl.pallas_call(functools.partial(kernel, steps, nlat, nlon), out_shape=ja...]
    unnamed x11 -> x1, local copies, waits for them, and re-layouts: 5.61 us -> 1.87 us
where the time goes in v2:
time: 66.6 us; the launch traced here: 66.5 us
  Pallas kernels  64.6 us (97%)
  local copies, waits for them, and re-layouts  1.87 us (3%)
    pallas_call x1, Pallas kernels, on_device(): pl.pallas_call(functools.partial(kernel, steps, nlat, nlon), out_shape=ja...  64.6 us
    unnamed x1, local copies, waits for them, and re-layouts  1.87 us

profile of v2, /device:TPU:1, one launch (start us, length us, event | category | flops | bytes accessed | tf_op | source)
XLA Modules:
  0.0 66.5 jit_solution(10055412782361134069)
XLA Ops:
  0.0 64.6 %shard_map.55 = f32[1024,128]{1,0:T(8,128)} custom-call(f32[1024,128]{1,0:T(8,128)} %bitcast.7, f32[64,2,8,128]{3,2,1,0:T(8,128)} %bitcast.8, f32[1024,128]{1,0:T(8,128)} %bitcast.9, s32[1024,128]{1,0:T(8,128)} %bitcast.10, f32[1024,128]{1,0:T(8,128)} %bitcast.11, f32[8]{0:T(128)} %table_ref.1), custom_call_target="tpu_custom_call" | custom-call | tf_op jit(solution)/shard_map/pallas_call | solution.py:636
  64.6 1.9 %copy.7 = f32[1,64,16,128]{3,2,1,0:T(8,128)} copy(f32[1,64,16,128]{3,2,1,0:T(8,128)} %bitcast.6) | data formatting | bytes 1048576

commit v3 on v2

--- a/solution.py
+++ b/solution.py
@@ -13,10 +13,11 @@
 CORNER = 0.1
 SWEEPS = 3
 LP = 8
+GROUPS = 2
 AP = 8
 NA = 16
 NX = 128
-VMEM_LIMIT = 62 * 1024 * 1024
+VMEM_LIMIT = 40 * 1024 * 1024
 
 
 def harmonic(first, second):
@@ -76,10 +77,10 @@
 
 def kernel(
     steps, nlat, nlon,
-    u_hbm, u_parts, h_hbm, reg_hbm, init_hbm, table_ref, out_ref,
-    u_ref, h_ref, reg_ref, kap, wts, pbuf, lat_out, lat_in, lon_out, lon_in, lon_mix,
-    rs, rr, ur, spec, coef, xe, xf, edge_out, edge_in, ws, wb,
-    local, shift_s, shift_r, side_s, side_r, state_s, state_r, fwd_s, fwd_r,
+    u_hbm, u_parts, h_hbm, reg_hbm, init_hbm, table_hbm, out_ref,
+    table_ref, u_ref, h_ref, reg_ref, kap, wts, pbuf, lat_out, lat_in, lon_out, lon_in, lon_mix,
+    rs, rr, ur, relay, spec, coef, xe, xf, edge_out, edge_in, ws, wb,
+    local, shift_s, shift_r, side_s, side_r, relay_s, relay_r, state_s, state_r, fwd_s, fwd_r,
     lev_s, lev_r, lat_s, lat_r, lon_s, lon_r, back_s, back_r,
 ):
     levels = u_ref.shape[0] // NA
@@ -140,6 +141,8 @@
     take_u = pltpu.make_async_copy(u_hbm, u_ref, local.at[1])
     take_h = pltpu.make_async_copy(h_hbm, h_ref, local.at[2])
     take_init = pltpu.make_async_copy(init_hbm, pbuf, local.at[3])
+    take_table = pltpu.make_async_copy(table_hbm, table_ref, local.at[4])
+    take_table.start()
     take_reg.start()
     take_u.start()
     take_h.start()
@@ -174,6 +177,7 @@
 
     kap[pl.ds(0, NA), :] = jnp.zeros((NA, NX), F32)
     kap[pl.ds((levels + 1) * NA, NA), :] = jnp.zeros((NA, NX), F32)
+    take_table.wait()
     table = [table_ref[c] for c in range(8)]
     take_reg.wait()
     take_u.wait()
@@ -234,26 +238,49 @@
         for i in range(zs):
             shift_copy(i).start()
 
-    def state_copy(to):
-        part = lax.rem(lax.rem(to, 2) + lat, 2)
-        return remote(
-            u_parts.at[pl.ds(lax.div(to, 2) * LP, LP), part], ur.at[z], state_s.at[to], state_r.at[z], {"tm": to}
-        )
-
-    sends_state = jnp.logical_and(xl == 1, z < zs - 1)
-
-    @pl.when(sends_state)
-    def _():
-        def send(i, carry):
-            odd = lax.rem(i, 2)
-            d = half + (1 - odd) * lax.div(i, 2) - odd * lax.div(i + 1, 2)
-            state_copy(lax.rem(me + d, steps)).start()
-            return carry
-
-        lax.fori_loop(0, steps - 1, send, 0)
+    sends_state = z < zs - 1
+
+    def state_parts(i, x):
+        return u_parts.at[pl.ds(order(i, z) * LP, LP), lax.rem(x + lat, 2)]
+
+    def relay_copy(i):
+        return remote(state_parts(i, 0), relay.at[i], relay_s.at[i], relay_r.at[i], {"tm": me + 1 - 2 * xl})
+
+    def state_copy(i):
+        to = order(i, z) * 2 + 1
+        return remote(state_parts(i, 1), ur.at[z], state_s.at[i], state_r.at[z], {"tm": to})
+
+    def forward_copy(i):
+        return remote(relay.at[i], ur.at[z], state_s.at[i], state_r.at[z], {"tm": order(i, z) * 2})
+
+    @pl.when(jnp.logical_and(xl == 1, sends_state))
+    def _():
+        for i in range(zs):
+            relay_copy(i).start()
+            if i < zs - 1:
+                state_copy(i).start()
         for l in range(LP):
             row = pl.multiple_of((z * LP + l) * NA + q * 8, 8)
             ur[z, l] = u_ref[pl.ds(row, 8), :]
+
+    def forward(i):
+        relay_copy(i).wait_recv()
+
+        @pl.when(i < zs - 1)
+        def _():
+            forward_copy(i).start()
+
+        @pl.when(i == zs - 1)
+        def _():
+            ur[z] = relay[i]
+
+    forwards = jnp.logical_and(xl == 0, sends_state)
+    ahead = min(2, zs - 1)
+
+    @pl.when(forwards)
+    def _():
+        for i in range(ahead):
+            forward(i)
 
     take_h.wait()
 
@@ -277,6 +304,10 @@
 
     def chunk(i, carry):
         zd = order(i, z)
+
+        @pl.when(jnp.logical_and(forwards, i + ahead < zs))
+        def _():
+            forward(i + ahead)
 
         @pl.when(xl == 1)
         def _():
@@ -378,9 +409,9 @@
     lax.fori_loop(1, steps, await_fwd, 0)
     for i in range(zs - 1):
 
-        @pl.when(me != 2 * i + 1)
+        @pl.when(z != i)
         def _():
-            remote(u_parts.at[pl.ds(0, LP), 0], ur.at[i], state_s.at[i], state_r.at[i], {"tm": 2 * i + 1}).wait_recv()
+            remote(relay.at[0], ur.at[i], state_s.at[i], state_r.at[i], {"tm": 2 * i + xl}).wait_recv()
 
     def sent_index(m, s):
         return 2 + 2 * m + s
@@ -400,8 +431,8 @@
         def __init__(self):
             self.parts = [zero, zero]
 
-        def add(self, s, a, f, tile):
-            j = (s * AP + a) * 2 + f
+        def add(self, p, a, f, tile):
+            j = (p * AP + a) * 2 + f
             self.parts[f] = jnp.where(lane_pair == j, pltpu.roll(tile, 2 * j + 1, 1), self.parts[f])
 
         def value(self):
@@ -418,14 +449,14 @@
         return remote(xe.at[b, 2 + d, inner], xe.at[b, d, inner], lev_s.at[b, d], lev_r.at[b, d], lev_sides[d][1])
 
     def lat_copy(b, m, d):
-        pair = pl.ds(2 + 2 * m, 2)
+        pair = pl.ds(2 + 4 * m, 4)
         return remote(
             xe.at[b, pair, 1 + d * (AP - 1)], xe.at[b, pair, (1 - d) * (AP + 1)],
             lat_s.at[b, m, d], lat_r.at[b, m, 1 - d], lat_sides[d][1],
         )
 
     def lat_arrival(b, m, d):
-        pair = pl.ds(2 + 2 * m, 2)
+        pair = pl.ds(2 + 4 * m, 4)
         return remote(
             xe.at[b, pair, 1 + d * (AP - 1)], xe.at[b, pair, d * (AP + 1)],
             lat_s.at[b, m, d], lat_r.at[b, m, d], lat_sides[d][1],
@@ -463,10 +494,12 @@
         for d in range(2):
             lon_arrival(b, m, d).wait_recv()
 
-    def to_spectrum(m, carry):
+    members = ((0, 0), (0, 1), (1, 0), (1, 1))
+
+    def to_spectrum(g, carry):
         packed = Packed()
-        for s in range(2):
-            l = level_of(m, s)
+        for mm, s in members:
+            l = level_of(2 * g + mm, s)
             at = pl.multiple_of(l * 8, 8)
             r = [rr[n, pl.ds(at, 8), :] for n in range(steps)]
             for n in range(2, steps, 2):
@@ -480,31 +513,32 @@
             spec[pl.ds(l * 128 + 8, 8, stride=16), :] = real[half]
             for k in range(1, half):
                 spec[pl.ds(l * 128 + 8 + k, 8, stride=16), :] = -imag[k - 1]
-        for s in range(2):
+        for p, (mm, s) in enumerate(members):
+            m = 2 * g + mm
             l = level_of(m, s)
             for a in range(AP):
                 row = pl.multiple_of((l * 8 + a) * 16, 8)
                 x = divide(l, a, spec[pl.ds(row, 8), :], spec[pl.ds(row + 8, 8), :])
                 for f in range(2):
                     xe[0, sent_index(m, s), a + 1, pl.ds(8 * f, 8), :] = x[f]
-                    packed.add(s, a, f, x[f])
-        send_edges(0, m, packed)
+                    packed.add(p, a, f, x[f])
+        send_edges(0, g, packed)
         return carry
 
-    lax.fori_loop(0, LP // 2, to_spectrum, 0)
+    lax.fori_loop(0, GROUPS, to_spectrum, 0)
 
     def back_copy(to, first, count):
         part = pl.ds(pl.multiple_of(first, 8), count)
         return remote(ws.at[to, part], wb.at[me, part], back_s.at[to], back_r.at[me], {"tm": to})
 
-    def from_spectrum(m, s):
-        base = s * 128
+    def from_spectrum(g, p):
+        base = p * 128
         x = [xf[pl.ds(base + k, 8, stride=16), :] for k in range(half)]
         x_half = xf[pl.ds(base + 8, 8, stride=16), :]
         y = [xf[pl.ds(base + 8 + k, 8, stride=16), :] for k in range(1, half)]
         even = cosine_sums([x[0] * 0.5] + x[1:] + [x_half * 0.5], steps)
         odd = sine_sums(y, steps)
-        at = pl.ds(pl.multiple_of(m * 16, 8) + s * 8, 8)
+        at = pl.ds(pl.multiple_of(g * 32, 8) + p * 8, 8)
         ws[0, at, :] = even[0]
         ws[half, at, :] = even[half]
         for n in range(1, half):
@@ -512,11 +546,12 @@
             ws[steps - n, at, :] = even[n] + odd[n - 1]
 
     def sweep(b, last):
-        def pair(m, carry):
-            await_edges(b, m)
-            ends = jnp.where(odd_lane, edge_in[b, m, 1], edge_in[b, m, 0])
+        def some_pairs(g, carry):
+            await_edges(b, g)
+            ends = jnp.where(odd_lane, edge_in[b, g, 1], edge_in[b, g, 0])
             packed = Packed()
-            for s in range(2):
+            for p, (mm, s) in enumerate(members):
+                m = 2 * g + mm
                 l = level_of(m, s)
                 i = sent_index(m, s)
                 beyond = (i - 2, inner_index(m, s))
@@ -529,7 +564,7 @@
                     rhs = []
                     for f in range(2):
                         part = pl.ds(8 * f, 8)
-                        j = (s * AP + a) * 2 + f
+                        j = (p * AP + a) * 2 + f
                         x = xe[b, i, a + 1, part, :]
                         halo = pltpu.roll(ends, NX - 1 - 2 * j, 1)
                         total = spec[pl.ds(row + 8 * f, 8), :]
@@ -541,29 +576,26 @@
                     x = divide(l, a, rhs[0], rhs[1])
                     for f in range(2):
                         if last:
-                            xf[pl.ds((s * AP + a) * 16 + 8 * f, 8), :] = x[f]
+                            xf[pl.ds((p * AP + a) * 16 + 8 * f, 8), :] = x[f]
                         else:
                             xe[b + 1, i, a + 1, pl.ds(8 * f, 8), :] = x[f]
-                            packed.add(s, a, f, x[f])
+                            packed.add(p, a, f, x[f])
             if not last:
-                send_edges(b + 1, m, packed)
+                send_edges(b + 1, g, packed)
             else:
-                for s in range(2):
-                    from_spectrum(m, s)
-
-                @pl.when(lax.rem(m, 2) == 1)
-                def _():
-                    def send(i, carry):
-                        odd = lax.rem(i, 2)
-                        d = half + (1 - odd) * lax.div(i, 2) - odd * lax.div(i + 1, 2)
-                        back_copy(lax.rem(me + d, steps), (m - 1) * 16, 32).start()
-                        return carry
-
-                    lax.fori_loop(0, steps - 1, send, 0)
-
+                for p in range(4):
+                    from_spectrum(g, p)
+
+                def send(i, carry):
+                    odd = lax.rem(i, 2)
+                    d = half + (1 - odd) * lax.div(i, 2) - odd * lax.div(i + 1, 2)
+                    back_copy(lax.rem(me + d, steps), g * 32, 32).start()
+                    return carry
+
+                lax.fori_loop(0, steps - 1, send, 0)
             return carry
 
-        lax.fori_loop(0, LP // 2, pair, 0)
+        lax.fori_loop(0, GROUPS, some_pairs, 0)
 
     for b in range(SWEEPS):
         sweep(b, b == SWEEPS - 1)
@@ -602,14 +634,20 @@
         to = lax.rem(me + d, steps)
         fwd_copy(0, 0, to).wait_send()
         back_copy(to, 0, 64).wait_send()
-
-        @pl.when(sends_state)
-        def _():
-            state_copy(to).wait_send()
-
         return carry
 
     lax.fori_loop(1, steps, sent, 0)
+
+    @pl.when(sends_state)
+    def _():
+        for i in range(zs - 1):
+            forward_copy(i).wait_send()
+
+    @pl.when(jnp.logical_and(xl == 1, sends_state))
+    def _():
+        for i in range(zs):
+            relay_copy(i).wait_send()
+
     for b in range(SWEEPS):
         for d in range(2):
             guarded(lev_sides[d][0], lambda b=b, d=d: lev_copy(b, d).wait_send())
@@ -620,7 +658,7 @@
                 lon_copy(b, m, d).wait_send()
             return carry
 
-        lax.fori_loop(0, LP // 2, edges_sent, 0)
+        lax.fori_loop(0, GROUPS, edges_sent, 0)
 
 
 def on_device(steps, nlat, nlon, iterate, heating, initial, region, cond_table):
@@ -628,7 +666,6 @@
     rows = levels * NA
     zs = steps // 2
     groups = (levels + 31) // 32
-    pairs = LP // 2
     vmem = pl.BlockSpec(memory_space=pltpu.VMEM)
     anywhere = pl.BlockSpec(memory_space=pl.ANY)
     flat = lambda value: value.reshape(rows, NX)
@@ -636,9 +673,10 @@
     out = pl.pallas_call(
         functools.partial(kernel, steps, nlat, nlon),
         out_shape=jax.ShapeDtypeStruct((rows, NX), F32),
-        in_specs=[anywhere] * 5 + [pl.BlockSpec(memory_space=pltpu.SMEM)],
+        in_specs=[anywhere] * 6,
         out_specs=vmem,
         scratch_shapes=[
+            pltpu.SMEM(cond_table.shape, F32),
             pltpu.VMEM((rows, NX), F32),
             pltpu.VMEM((rows, NX), F32),
             pltpu.VMEM((rows, NX), jnp.int32),
@@ -653,36 +691,44 @@
             pltpu.VMEM((2, levels * 8, NX), F32),
             pltpu.VMEM((steps, 64, NX), F32),
             pltpu.VMEM((zs, LP, 8, NX), F32),
+            pltpu.VMEM((zs, LP, 8, NX), F32),
             pltpu.VMEM((64 * 16, NX), F32),
             pltpu.VMEM((64 * 24, NX), F32),
             pltpu.VMEM((SWEEPS, LP + 2, AP + 2, 16, NX), F32),
-            pltpu.VMEM((16 * 16, NX), F32),
-            pltpu.VMEM((SWEEPS, pairs, 8, NX), F32),
-            pltpu.VMEM((SWEEPS, pairs, 2, 8, NX), F32),
+            pltpu.VMEM((32 * 16, NX), F32),
+            pltpu.VMEM((SWEEPS, GROUPS, 8, NX), F32),
+            pltpu.VMEM((SWEEPS, GROUPS, 2, 8, NX), F32),
             pltpu.VMEM((steps, 64, NX), F32),
             pltpu.VMEM((steps, 64, NX), F32),
-            dma((4,)),
+            dma((5,)),
             dma((zs,)),
             dma((zs,)),
             dma((4,)),
             dma((4,)),
-            dma((steps,)),
+            dma((zs,)),
+            dma((zs,)),
+            dma((zs,)),
             dma((zs,)),
             dma((steps,)),
             dma((steps,)),
             dma((SWEEPS, 2)),
             dma((SWEEPS, 2)),
-            dma((SWEEPS, pairs, 2)),
-            dma((SWEEPS, pairs, 2)),
-            dma((SWEEPS, pairs, 2)),
-            dma((SWEEPS, pairs, 2)),
+            dma((SWEEPS, GROUPS, 2)),
+            dma((SWEEPS, GROUPS, 2)),
+            dma((SWEEPS, GROUPS, 2)),
+            dma((SWEEPS, GROUPS, 2)),
             dma((steps,)),
             dma((steps,)),
         ],
         compiler_params=pltpu.CompilerParams(
             collective_id=0, has_side_effects=True, vmem_limit_bytes=VMEM_LIMIT
         ),
-    )(flat(iterate), iterate.reshape(levels, 2, AP, NX), flat(heating), flat(region), flat(initial), cond_table)
+    )(*(
+        pltpu.with_memory_space_constraint(value, pltpu.HBM)
+        for value in (
+            flat(iterate), iterate.reshape(levels, 2, AP, NX), flat(heating), flat(region), flat(initial), cond_table
+        )
+    ))
     return out.reshape(iterate.shape)
 
 

time: 66.6 us -> 62.3 us (0.935)
  Pallas kernels: 64.6 us -> 61.4 us
  local copies, waits for them, and re-layouts: 1.87 us -> 0.8 us
    pallas_call x1, Pallas kernels: 64.6 us -> 61.4 us  [on_device(): pl.pallas_call(functools.partial(kernel, steps, nlat, nlon), out_shape=ja...]
    unnamed x1, local copies, waits for them, and re-layouts: 1.87 us -> 0.8 us
where the time goes in v3:
time: 62.3 us; the launch traced here: 62.2 us
  Pallas kernels  61.4 us (99%)
  local copies, waits for them, and re-layouts  0.8 us (1%)
    pallas_call x1, Pallas kernels, on_device(): pl.pallas_call(functools.partial(kernel, steps, nlat, nlon), out_shape=ja...  61.4 us

profile of v3, /device:TPU:1, one launch (start us, length us, event | category | flops | bytes accessed | tf_op | source)
XLA Modules:
  0.0 62.2 jit_solution(15309997434591158128)
XLA Ops:
  0.0 61.4 %shard_map.55 = f32[1024,128]{1,0:T(8,128)S(1)} custom-call(f32[1024,128]{1,0:T(8,128)} %bitcast.7, f32[64,2,8,128]{3,2,1,0:T(8,128)} %bitcast.8, f32[1024,128]{1,0:T(8,128)} %bitcast.9, s32[1024,128]{1,0:T(8,128)} %bitcast.10, f32[1024,128]{1,0:T(8,128)} %bitcast.11, f32[8]{0:T(128)} %table_hbm.1), custom_call_target="tpu_custom_call" | custom-call | tf_op jit(solution)/shard_map/pallas_call | solution.py:673
  61.4 0.8 %copy.7 = f32[1,64,16,128]{3,2,1,0:T(8,128)} copy(f32[1,64,16,128]{3,2,1,0:T(8,128)S(1)} %bitcast.6) | data formatting | bytes 1048576

commit v4 on v3

--- a/solution.py
+++ b/solution.py
@@ -78,12 +78,13 @@
 def kernel(
     steps, nlat, nlon,
     u_hbm, u_parts, h_hbm, reg_hbm, init_hbm, table_hbm, out_ref,
-    table_ref, u_ref, h_ref, reg_ref, kap, wts, pbuf, lat_out, lat_in, lon_out, lon_in, lon_mix,
-    rs, rr, ur, relay, spec, coef, xe, xf, edge_out, edge_in, ws, wb,
+    table_ref, u_ref, h_ref, reg_ref, kap, wts, own, pbuf, lat_out, lat_in, lon_out, lon_in, lon_mix,
+    rs, rr, ur, relay, spec, coef, xe0, xe1, xe2, xf, edge_out, edge_in, ws, wb,
     local, shift_s, shift_r, side_s, side_r, relay_s, relay_r, state_s, state_r, fwd_s, fwd_r,
     lev_s, lev_r, lat_s, lat_r, lon_s, lon_r, back_s, back_r,
 ):
     levels = u_ref.shape[0] // NA
+    xe = (xe0, xe1, xe2)
     zs = steps // 2
     half = steps // 2
     me = lax.axis_index("tm")
@@ -159,7 +160,7 @@
             ((1 - q) + (nlat - 1 - lat) == 0, (b, slice(None), AP + 1)),
         ):
             def clear(place=place):
-                xe[place] = jnp.zeros((10, 16, NX), F32)
+                xe[place[0]][place[1:]] = jnp.zeros((10, 16, NX), F32)
 
             pl.when(condition)(clear)
 
@@ -201,26 +202,38 @@
         packs = lax.fori_loop(0, min(4, levels // 8 - 4 * group), conduct, (zero, zero))
         for f in range(2):
             lon_out[group, f] = packs[f]
-    for g in range(levels // 8):
+    for g in range(zs):
+        e = lax.rem(g + zs - z, zs) - zs // 2
+        at = pl.multiple_of(jnp.where(e < 0, -2 * e - 1, 2 * e) * 16, 8)
         for side, row in ((0, 0), (1, NA - 1)):
-            lat_out[side, pl.ds(g * 8, 8), :] = u_ref[pl.ds(g * 128 + row, 8, stride=NA), :]
-            lat_out[side, pl.ds(levels + g * 8, 8), :] = kap[pl.ds(NA + g * 128 + row, 8, stride=NA), :]
+            lat_out[side, pl.ds(at, 8), :] = u_ref[pl.ds(g * 128 + row, 8, stride=NA), :]
+            lat_out[side, pl.ds(at + 8, 8), :] = kap[pl.ds(NA + g * 128 + row, 8, stride=NA), :]
 
     lat_count = jnp.where(lat > 0, 1, 0) + jnp.where(lat < nlat - 1, 1, 0)
     pl.semaphore_wait(barrier, steps - 1 + 2 + lat_count)
 
+    def lat_rows(d):
+        return pl.ds(0, 16) if d < 2 else pl.ds(16, 2 * levels - 16)
+
     def side_copy(d):
-        if d < 2:
-            return remote(lat_out.at[d], lat_in.at[1 - d], side_s.at[d], side_r.at[1 - d], sides[d][1])
-        return remote(lon_out, lon_in.at[3 - d], side_s.at[d], side_r.at[5 - d], sides[d][1])
+        if d in (2, 3):
+            return remote(lon_out, lon_in.at[3 - d], side_s.at[d], side_r.at[5 - d], sides[d][1])
+        e = d % 2
+        return remote(
+            lat_out.at[e, lat_rows(d)], lat_in.at[1 - e, lat_rows(d)], side_s.at[d], side_r.at[d + 1 - 2 * e], sides[e][1]
+        )
 
     def side_arrival(d):
-        if d < 2:
-            return remote(lat_out.at[d], lat_in.at[d], side_s.at[d], side_r.at[d], sides[d][1])
-        return remote(lon_out, lon_in.at[d - 2], side_s.at[d], side_r.at[d], sides[d][1])
-
-    for d in range(4):
-        guarded(sides[d][0], lambda d=d: side_copy(d).start())
+        if d in (2, 3):
+            return remote(lon_out, lon_in.at[d - 2], side_s.at[d], side_r.at[d], sides[d][1])
+        e = d % 2
+        return remote(lat_out.at[e, lat_rows(d)], lat_in.at[e, lat_rows(d)], side_s.at[d], side_r.at[d], sides[e][1])
+
+    def side_there(d):
+        return None if d in (2, 3) else sides[d % 2][0]
+
+    for d in (2, 3, 0, 1, 4, 5):
+        guarded(side_there(d), lambda d=d: side_copy(d).start())
 
     def order(i, at):
         odd = lax.rem(i, 2)
@@ -239,6 +252,7 @@
             shift_copy(i).start()
 
     sends_state = z < zs - 1
+    relayed = min(4, zs // 2 + 0)
 
     def state_parts(i, x):
         return u_parts.at[pl.ds(order(i, z) * LP, LP), lax.rem(x + lat, 2)]
@@ -250,38 +264,33 @@
         to = order(i, z) * 2 + 1
         return remote(state_parts(i, 1), ur.at[z], state_s.at[i], state_r.at[z], {"tm": to})
 
+    def direct_copy(i):
+        return remote(state_parts(i, 0), ur.at[z], relay_s.at[i], state_r.at[z], {"tm": order(i, z) * 2})
+
     def forward_copy(i):
         return remote(relay.at[i], ur.at[z], state_s.at[i], state_r.at[z], {"tm": order(i, z) * 2})
 
     @pl.when(jnp.logical_and(xl == 1, sends_state))
     def _():
         for i in range(zs):
-            relay_copy(i).start()
+            if i < relayed:
+                relay_copy(i).start()
             if i < zs - 1:
                 state_copy(i).start()
+            if i >= relayed:
+                direct_copy(i).start()
         for l in range(LP):
             row = pl.multiple_of((z * LP + l) * NA + q * 8, 8)
             ur[z, l] = u_ref[pl.ds(row, 8), :]
 
-    def forward(i):
-        relay_copy(i).wait_recv()
-
-        @pl.when(i < zs - 1)
-        def _():
+    forwards = jnp.logical_and(xl == 0, sends_state)
+
+    @pl.when(forwards)
+    def _():
+        for i in range(relayed):
+            relay_copy(i).wait_recv()
             forward_copy(i).start()
 
-        @pl.when(i == zs - 1)
-        def _():
-            ur[z] = relay[i]
-
-    forwards = jnp.logical_and(xl == 0, sends_state)
-    ahead = min(2, zs - 1)
-
-    @pl.when(forwards)
-    def _():
-        for i in range(ahead):
-            forward(i)
-
     take_h.wait()
 
     @pl.when(me == 0)
@@ -289,7 +298,7 @@
         take_init.wait()
 
     for d in range(4):
-        guarded(sides[d][0], lambda d=d: side_arrival(d).wait_recv())
+        guarded(side_there(d), lambda d=d: side_arrival(d).wait_recv())
     for group in range((levels + 31) // 32):
         for f in range(2):
             lon_mix[group, f] = jnp.where(odd_lane, lon_in[1, group, f], lon_in[0, group, f])
@@ -305,9 +314,10 @@
     def chunk(i, carry):
         zd = order(i, z)
 
-        @pl.when(jnp.logical_and(forwards, i + ahead < zs))
+        @pl.when(i == 1)
         def _():
-            forward(i + ahead)
+            for d in (4, 5):
+                guarded(side_there(d), lambda d=d: side_arrival(d).wait_recv())
 
         @pl.when(xl == 1)
         def _():
@@ -328,7 +338,7 @@
                 down = [ref[pl.ds(low + 8 * t, 8), :] for t in range(2)]
                 up = [ref[pl.ds(high + 8 * t, 8), :] for t in range(2)]
                 row = [
-                    jnp.broadcast_to(lat_in[s, pl.ds(f * levels + lev, 1), :], (8, NX)) for s in range(2)
+                    jnp.broadcast_to(lat_in[s, pl.ds(i * 16 + f * 8 + l, 1), :], (8, NX)) for s in range(2)
                 ]
                 one = [pltpu.roll(tile[t], 1, 0) for t in range(2)]
                 seven = [pltpu.roll(tile[t], 7, 0) for t in range(2)]
@@ -380,9 +390,11 @@
 
     def invert(l, carry):
         at = pl.multiple_of(l * NA + q * 8, 8)
-        total = wts[0, pl.ds(at, 8), :]
-        for f in range(1, 6):
-            total = total + wts[f, pl.ds(at, 8), :]
+        total = None
+        for f in range(6):
+            w = wts[f, pl.ds(at, 8), :]
+            own[f, l] = w
+            total = w if total is None else total + w
         for k in range(half + 1):
             re = total + shift_re[k]
             if k in (0, half):
@@ -409,7 +421,7 @@
     lax.fori_loop(1, steps, await_fwd, 0)
     for i in range(zs - 1):
 
-        @pl.when(z != i)
+        @pl.when(jnp.logical_or(z != i, xl == 0))
         def _():
             remote(relay.at[0], ur.at[i], state_s.at[i], state_r.at[i], {"tm": 2 * i + xl}).wait_recv()
 
@@ -442,23 +454,23 @@
 
     def lev_copy(b, d):
         return remote(
-            xe.at[b, 2 + d, inner], xe.at[b, 1 - d, inner], lev_s.at[b, d], lev_r.at[b, 1 - d], lev_sides[d][1]
+            xe[b].at[2 + d, inner], xe[b].at[1 - d, inner], lev_s.at[b, d], lev_r.at[b, 1 - d], lev_sides[d][1]
         )
 
     def lev_arrival(b, d):
-        return remote(xe.at[b, 2 + d, inner], xe.at[b, d, inner], lev_s.at[b, d], lev_r.at[b, d], lev_sides[d][1])
+        return remote(xe[b].at[2 + d, inner], xe[b].at[d, inner], lev_s.at[b, d], lev_r.at[b, d], lev_sides[d][1])
 
     def lat_copy(b, m, d):
         pair = pl.ds(2 + 4 * m, 4)
         return remote(
-            xe.at[b, pair, 1 + d * (AP - 1)], xe.at[b, pair, (1 - d) * (AP + 1)],
+            xe[b].at[pair, 1 + d * (AP - 1)], xe[b].at[pair, (1 - d) * (AP + 1)],
             lat_s.at[b, m, d], lat_r.at[b, m, 1 - d], lat_sides[d][1],
         )
 
     def lat_arrival(b, m, d):
         pair = pl.ds(2 + 4 * m, 4)
         return remote(
-            xe.at[b, pair, 1 + d * (AP - 1)], xe.at[b, pair, d * (AP + 1)],
+            xe[b].at[pair, 1 + d * (AP - 1)], xe[b].at[pair, d * (AP + 1)],
             lat_s.at[b, m, d], lat_r.at[b, m, d], lat_sides[d][1],
         )
 
@@ -473,15 +485,16 @@
     def send_edges(b, m, packed):
         edge_out[b, m] = packed.value()
 
+        for d in range(2):
+            lon_copy(b, m, d).start()
+        for d in range(2):
+            guarded(lat_sides[d][0], lambda d=d: lat_copy(b, m, d).start())
+
+    def send_levels(b, m):
         @pl.when(m == 0)
         def _():
             for d in range(2):
                 guarded(lev_sides[d][0], lambda d=d: lev_copy(b, d).start())
-
-        for d in range(2):
-            lon_copy(b, m, d).start()
-        for d in range(2):
-            guarded(lat_sides[d][0], lambda d=d: lat_copy(b, m, d).start())
 
     def await_edges(b, m):
         @pl.when(m == 0)
@@ -520,8 +533,10 @@
                 row = pl.multiple_of((l * 8 + a) * 16, 8)
                 x = divide(l, a, spec[pl.ds(row, 8), :], spec[pl.ds(row + 8, 8), :])
                 for f in range(2):
-                    xe[0, sent_index(m, s), a + 1, pl.ds(8 * f, 8), :] = x[f]
+                    xe[0][sent_index(m, s), a + 1, pl.ds(8 * f, 8), :] = x[f]
                     packed.add(p, a, f, x[f])
+            if p == 1:
+                send_levels(0, g)
         send_edges(0, g, packed)
         return carry
 
@@ -558,18 +573,18 @@
                 under, over = beyond if s == 0 else beyond[::-1]
                 for a in range(AP):
                     w = [
-                        jnp.broadcast_to(wts[f, pl.ds(l * NA + q * 8 + a, 1), :], (8, NX)) for f in range(6)
+                        jnp.broadcast_to(own[f, l, pl.ds(a, 1), :], (8, NX)) for f in range(6)
                     ]
                     row = pl.multiple_of((l * 8 + a) * 16, 8)
                     rhs = []
                     for f in range(2):
                         part = pl.ds(8 * f, 8)
                         j = (p * AP + a) * 2 + f
-                        x = xe[b, i, a + 1, part, :]
+                        x = xe[b][i, a + 1, part, :]
                         halo = pltpu.roll(ends, NX - 1 - 2 * j, 1)
                         total = spec[pl.ds(row + 8 * f, 8), :]
-                        total = total + w[0] * xe[b, under, a + 1, part, :] + w[1] * xe[b, over, a + 1, part, :]
-                        total = total + w[2] * xe[b, i, a, part, :] + w[3] * xe[b, i, a + 2, part, :]
+                        total = total + w[0] * xe[b][under, a + 1, part, :] + w[1] * xe[b][over, a + 1, part, :]
+                        total = total + w[2] * xe[b][i, a, part, :] + w[3] * xe[b][i, a + 2, part, :]
                         total = total + w[4] * pltpu.roll(jnp.where(last_lane, halo, x), 1, 1)
                         total = total + w[5] * pltpu.roll(jnp.where(first_lane, halo, x), NX - 1, 1)
                         rhs.append(total)
@@ -578,8 +593,10 @@
                         if last:
                             xf[pl.ds((p * AP + a) * 16 + 8 * f, 8), :] = x[f]
                         else:
-                            xe[b + 1, i, a + 1, pl.ds(8 * f, 8), :] = x[f]
+                            xe[b + 1][i, a + 1, pl.ds(8 * f, 8), :] = x[f]
                             packed.add(p, a, f, x[f])
+                if p == 1 and not last:
+                    send_levels(b + 1, g)
             if not last:
                 send_edges(b + 1, g, packed)
             else:
@@ -627,8 +644,8 @@
         for i in range(zs):
             shift_copy(i).wait_send()
 
-    for d in range(4):
-        guarded(sides[d][0], lambda d=d: side_copy(d).wait_send())
+    for d in range(6):
+        guarded(side_there(d), lambda d=d: side_copy(d).wait_send())
 
     def sent(d, carry):
         to = lax.rem(me + d, steps)
@@ -638,15 +655,17 @@
 
     lax.fori_loop(1, steps, sent, 0)
 
-    @pl.when(sends_state)
-    def _():
-        for i in range(zs - 1):
+    @pl.when(forwards)
+    def _():
+        for i in range(relayed):
             forward_copy(i).wait_send()
 
     @pl.when(jnp.logical_and(xl == 1, sends_state))
     def _():
         for i in range(zs):
             relay_copy(i).wait_send()
+            if i < zs - 1:
+                state_copy(i).wait_send()
 
     for b in range(SWEEPS):
         for d in range(2):
@@ -682,6 +701,7 @@
             pltpu.VMEM((rows, NX), jnp.int32),
             pltpu.VMEM((rows + 2 * NA, NX), F32),
             pltpu.VMEM((6, LP * NA, NX), F32),
+            pltpu.VMEM((6, LP, AP, NX), F32),
             pltpu.VMEM((rows, NX), F32),
             pltpu.VMEM((2, 2 * levels, NX), F32),
             pltpu.VMEM((2, 2 * levels, NX), F32),
@@ -694,7 +714,7 @@
             pltpu.VMEM((zs, LP, 8, NX), F32),
             pltpu.VMEM((64 * 16, NX), F32),
             pltpu.VMEM((64 * 24, NX), F32),
-            pltpu.VMEM((SWEEPS, LP + 2, AP + 2, 16, NX), F32),
+            *[pltpu.VMEM((LP + 2, AP + 2, 16, NX), F32) for _ in range(SWEEPS)],
             pltpu.VMEM((32 * 16, NX), F32),
             pltpu.VMEM((SWEEPS, GROUPS, 8, NX), F32),
             pltpu.VMEM((SWEEPS, GROUPS, 2, 8, NX), F32),
@@ -703,8 +723,8 @@
             dma((5,)),
             dma((zs,)),
             dma((zs,)),
-            dma((4,)),
-            dma((4,)),
+            dma((6,)),
+            dma((6,)),
             dma((zs,)),
             dma((zs,)),
             dma((zs,)),

time: 62.3 us -> 60.5 us (0.971)
  Pallas kernels: 61.4 us -> 59.6 us
    pallas_call x1, Pallas kernels: 61.4 us -> 59.6 us  [on_device(): pl.pallas_call(functools.partial(kernel, steps, nlat, nlon), out_shape=ja...]
where the time goes in v4:
time: 60.5 us; the launch traced here: 60.4 us
  Pallas kernels  59.6 us (99%)
  local copies, waits for them, and re-layouts  0.8 us (1%)
    pallas_call x1, Pallas kernels, on_device(): pl.pallas_call(functools.partial(kernel, steps, nlat, nlon), out_shape=ja...  59.6 us

profile of v4, /device:TPU:1, one launch (start us, length us, event | category | flops | bytes accessed | tf_op | source)
XLA Modules:
  0.0 60.4 jit_solution(8845555746949368490)
XLA Ops:
  0.0 59.6 %shard_map.55 = f32[1024,128]{1,0:T(8,128)S(1)} custom-call(f32[1024,128]{1,0:T(8,128)} %bitcast.7, f32[64,2,8,128]{3,2,1,0:T(8,128)} %bitcast.8, f32[1024,128]{1,0:T(8,128)} %bitcast.9, s32[1024,128]{1,0:T(8,128)} %bitcast.10, f32[1024,128]{1,0:T(8,128)} %bitcast.11, f32[8]{0:T(128)} %table_hbm.1), custom_call_target="tpu_custom_call" | custom-call | tf_op jit(solution)/shard_map/pallas_call | solution.py:692
  59.6 0.8 %copy.7 = f32[1,64,16,128]{3,2,1,0:T(8,128)} copy(f32[1,64,16,128]{3,2,1,0:T(8,128)S(1)} %bitcast.6) | data formatting | bytes 1048576

commit v5 on v4

--- a/solution.py
+++ b/solution.py
@@ -79,12 +79,13 @@
     steps, nlat, nlon,
     u_hbm, u_parts, h_hbm, reg_hbm, init_hbm, table_hbm, out_ref,
     table_ref, u_ref, h_ref, reg_ref, kap, wts, own, pbuf, lat_out, lat_in, lon_out, lon_in, lon_mix,
-    rs, rr, ur, relay, spec, coef, xe0, xe1, xe2, xf, edge_out, edge_in, ws, wb,
+    rs, rr, ur, relay, spec, coef, xe0, xe1, xe2, rot0, rot1, rot2, xf, edge_out, edge_in, ws, wb,
     local, shift_s, shift_r, side_s, side_r, relay_s, relay_r, state_s, state_r, fwd_s, fwd_r,
     lev_s, lev_r, lat_s, lat_r, lon_s, lon_r, back_s, back_r,
 ):
     levels = u_ref.shape[0] // NA
     xe = (xe0, xe1, xe2)
+    rot = (rot0, rot1, rot2)
     zs = steps // 2
     half = steps // 2
     me = lax.axis_index("tm")
@@ -439,13 +440,18 @@
         c_re, c_im, cross = (coef[pl.ds(at + 8 * i, 8), :] for i in range(3))
         return re * c_re - im * cross, im * c_im + re * cross
 
+    def turn(tile, by):
+        return tile if by % NX == 0 else pltpu.roll(tile, by % NX, 1)
+
     class Packed:
         def __init__(self):
             self.parts = [zero, zero]
 
         def add(self, p, a, f, tile):
             j = (p * AP + a) * 2 + f
-            self.parts[f] = jnp.where(lane_pair == j, pltpu.roll(tile, 2 * j + 1, 1), self.parts[f])
+            turned = pltpu.roll(tile, 2 * j + 1, 1)
+            self.parts[f] = jnp.where(lane_pair == j, turned, self.parts[f])
+            return turned
 
         def value(self):
             return jnp.where(lax.rem(lane_pair, 2) == 0, self.parts[0], self.parts[1])
@@ -534,7 +540,7 @@
                 x = divide(l, a, spec[pl.ds(row, 8), :], spec[pl.ds(row + 8, 8), :])
                 for f in range(2):
                     xe[0][sent_index(m, s), a + 1, pl.ds(8 * f, 8), :] = x[f]
-                    packed.add(p, a, f, x[f])
+                    rot[0][sent_index(m, s), a, pl.ds(8 * f, 8), :] = packed.add(p, a, f, x[f])
             if p == 1:
                 send_levels(0, g)
         send_edges(0, g, packed)
@@ -580,13 +586,13 @@
                     for f in range(2):
                         part = pl.ds(8 * f, 8)
                         j = (p * AP + a) * 2 + f
-                        x = xe[b][i, a + 1, part, :]
-                        halo = pltpu.roll(ends, NX - 1 - 2 * j, 1)
+                        turned = rot[b][i, a, part, :]
+                        west = jnp.where(lane == 2 * j, ends, turned)
+                        east = jnp.where(lane == 2 * j + 1, ends, turned)
                         total = spec[pl.ds(row + 8 * f, 8), :]
                         total = total + w[0] * xe[b][under, a + 1, part, :] + w[1] * xe[b][over, a + 1, part, :]
                         total = total + w[2] * xe[b][i, a, part, :] + w[3] * xe[b][i, a + 2, part, :]
-                        total = total + w[4] * pltpu.roll(jnp.where(last_lane, halo, x), 1, 1)
-                        total = total + w[5] * pltpu.roll(jnp.where(first_lane, halo, x), NX - 1, 1)
+                        total = total + w[4] * turn(west, NX - 2 * j) + w[5] * turn(east, NX - 2 * j - 2)
                         rhs.append(total)
                     x = divide(l, a, rhs[0], rhs[1])
                     for f in range(2):
@@ -594,7 +600,7 @@
                             xf[pl.ds((p * AP + a) * 16 + 8 * f, 8), :] = x[f]
                         else:
                             xe[b + 1][i, a + 1, pl.ds(8 * f, 8), :] = x[f]
-                            packed.add(p, a, f, x[f])
+                            rot[b + 1][i, a, pl.ds(8 * f, 8), :] = packed.add(p, a, f, x[f])
                 if p == 1 and not last:
                     send_levels(b + 1, g)
             if not last:
@@ -715,6 +721,7 @@
             pltpu.VMEM((64 * 16, NX), F32),
             pltpu.VMEM((64 * 24, NX), F32),
             *[pltpu.VMEM((LP + 2, AP + 2, 16, NX), F32) for _ in range(SWEEPS)],
+            *[pltpu.VMEM((LP + 2, AP, 16, NX), F32) for _ in range(SWEEPS)],
             pltpu.VMEM((32 * 16, NX), F32),
             pltpu.VMEM((SWEEPS, GROUPS, 8, NX), F32),
             pltpu.VMEM((SWEEPS, GROUPS, 2, 8, NX), F32),

time: 60.5 us -> 59.4 us (0.982)
  Pallas kernels: 59.6 us -> 58.5 us
    pallas_call x1, Pallas kernels: 59.6 us -> 58.5 us  [on_device(): pl.pallas_call(functools.partial(kernel, steps, nlat, nlon), out_shape=ja...]
where the time goes in v5:
time: 59.4 us; the launch traced here: 59.3 us
  Pallas kernels  58.5 us (98%)
  local copies, waits for them, and re-layouts  0.8 us (1%)
    pallas_call x1, Pallas kernels, on_device(): pl.pallas_call(functools.partial(kernel, steps, nlat, nlon), out_shape=ja...  58.5 us

profile of v5, /device:TPU:1, one launch (start us, length us, event | category | flops | bytes accessed | tf_op | source)
XLA Modules:
  0.0 59.3 jit_solution(8747323341385003098)
XLA Ops:
  0.0 58.5 %shard_map.55 = f32[1024,128]{1,0:T(8,128)S(1)} custom-call(f32[1024,128]{1,0:T(8,128)} %bitcast.7, f32[64,2,8,128]{3,2,1,0:T(8,128)} %bitcast.8, f32[1024,128]{1,0:T(8,128)} %bitcast.9, s32[1024,128]{1,0:T(8,128)} %bitcast.10, f32[1024,128]{1,0:T(8,128)} %bitcast.11, f32[8]{0:T(128)} %table_hbm.1), custom_call_target="tpu_custom_call" | custom-call | tf_op jit(solution)/shard_map/pallas_call | solution.py:698
  58.5 0.8 %copy.7 = f32[1,64,16,128]{3,2,1,0:T(8,128)} copy(f32[1,64,16,128]{3,2,1,0:T(8,128)S(1)} %bitcast.6) | data formatting | bytes 1048576

commit v6 on v5

--- a/solution.py
+++ b/solution.py
@@ -253,7 +253,7 @@
             shift_copy(i).start()
 
     sends_state = z < zs - 1
-    relayed = min(4, zs // 2 + 0)
+    relayed = min(5, zs // 2 + 1)
 
     def state_parts(i, x):
         return u_parts.at[pl.ds(order(i, z) * LP, LP), lax.rem(x + lat, 2)]
@@ -466,8 +466,8 @@
     def lev_arrival(b, d):
         return remote(xe[b].at[2 + d, inner], xe[b].at[d, inner], lev_s.at[b, d], lev_r.at[b, d], lev_sides[d][1])
 
-    def lat_copy(b, m, d):
-        pair = pl.ds(2 + 4 * m, 4)
+    def lat_copy(b, m, d, at=0, count=4):
+        pair = pl.ds(2 + 4 * m + at, count)
         return remote(
             xe[b].at[pair, 1 + d * (AP - 1)], xe[b].at[pair, (1 - d) * (AP + 1)],
             lat_s.at[b, m, d], lat_r.at[b, m, 1 - d], lat_sides[d][1],
@@ -494,9 +494,12 @@
         for d in range(2):
             lon_copy(b, m, d).start()
         for d in range(2):
-            guarded(lat_sides[d][0], lambda d=d: lat_copy(b, m, d).start())
+            guarded(lat_sides[d][0], lambda d=d: lat_copy(b, m, d, 2, 2).start())
 
     def send_levels(b, m):
+        for d in range(2):
+            guarded(lat_sides[d][0], lambda d=d: lat_copy(b, m, d, 0, 2).start())
+
         @pl.when(m == 0)
         def _():
             for d in range(2):

time: 59.4 us -> 59 us (level)
  no operation moved by 1% of the time
where the time goes in v6:
time: 59 us; the launch traced here: 58.9 us
  Pallas kernels  58.1 us (98%)
  local copies, waits for them, and re-layouts  0.8 us (1%)
    pallas_call x1, Pallas kernels, on_device(): pl.pallas_call(functools.partial(kernel, steps, nlat, nlon), out_shape=ja...  58.1 us

profile of v6, /device:TPU:1, one launch (start us, length us, event | category | flops | bytes accessed | tf_op | source)
XLA Modules:
  0.0 58.9 jit_solution(12434742977002944301)
XLA Ops:
  0.0 58.1 %shard_map.55 = f32[1024,128]{1,0:T(8,128)S(1)} custom-call(f32[1024,128]{1,0:T(8,128)} %bitcast.7, f32[64,2,8,128]{3,2,1,0:T(8,128)} %bitcast.8, f32[1024,128]{1,0:T(8,128)} %bitcast.9, s32[1024,128]{1,0:T(8,128)} %bitcast.10, f32[1024,128]{1,0:T(8,128)} %bitcast.11, f32[8]{0:T(128)} %table_hbm.1), custom_call_target="tpu_custom_call" | custom-call | tf_op jit(solution)/shard_map/pallas_call | solution.py:701
  58.1 0.8 %copy.7 = f32[1,64,16,128]{3,2,1,0:T(8,128)} copy(f32[1,64,16,128]{3,2,1,0:T(8,128)S(1)} %bitcast.6) | data formatting | bytes 1048576

commit v7 on v6

--- a/solution.py
+++ b/solution.py
@@ -626,6 +626,45 @@
     for b in range(SWEEPS):
         sweep(b, b == SWEEPS - 1)
 
+    @pl.when(xl == 0)
+    def _():
+        for i in range(zs):
+            shift_copy(i).wait_send()
+
+    for d in range(6):
+        guarded(side_there(d), lambda d=d: side_copy(d).wait_send())
+
+    def sent(d, carry):
+        to = lax.rem(me + d, steps)
+        fwd_copy(0, 0, to).wait_send()
+        return carry
+
+    lax.fori_loop(1, steps, sent, 0)
+
+    @pl.when(forwards)
+    def _():
+        for i in range(relayed):
+            forward_copy(i).wait_send()
+
+    @pl.when(jnp.logical_and(xl == 1, sends_state))
+    def _():
+        for i in range(zs):
+            relay_copy(i).wait_send()
+            if i < zs - 1:
+                state_copy(i).wait_send()
+
+    for b in range(SWEEPS):
+        for d in range(2):
+            guarded(lev_sides[d][0], lambda b=b, d=d: lev_copy(b, d).wait_send())
+
+        def edges_sent(m, carry, b=b):
+            for d in range(2):
+                guarded(lat_sides[d][0], lambda d=d: lat_copy(b, m, d).wait_send())
+                lon_copy(b, m, d).wait_send()
+            return carry
+
+        lax.fori_loop(0, GROUPS, edges_sent, 0)
+
     wb[me] = ws[me]
     share = pick(me, [2.0 / (steps * g) for g in gamma])
 
@@ -648,45 +687,11 @@
 
     lax.fori_loop(0, steps, finish, 0)
 
-    @pl.when(xl == 0)
-    def _():
-        for i in range(zs):
-            shift_copy(i).wait_send()
-
-    for d in range(6):
-        guarded(side_there(d), lambda d=d: side_copy(d).wait_send())
-
-    def sent(d, carry):
-        to = lax.rem(me + d, steps)
-        fwd_copy(0, 0, to).wait_send()
-        back_copy(to, 0, 64).wait_send()
+    def returned(d, carry):
+        back_copy(lax.rem(me + d, steps), 0, 64).wait_send()
         return carry
 
-    lax.fori_loop(1, steps, sent, 0)
-
-    @pl.when(forwards)
-    def _():
-        for i in range(relayed):
-            forward_copy(i).wait_send()
-
-    @pl.when(jnp.logical_and(xl == 1, sends_state))
-    def _():
-        for i in range(zs):
-            relay_copy(i).wait_send()
-            if i < zs - 1:
-                state_copy(i).wait_send()
-
-    for b in range(SWEEPS):
-        for d in range(2):
-            guarded(lev_sides[d][0], lambda b=b, d=d: lev_copy(b, d).wait_send())
-
-        def edges_sent(m, carry, b=b):
-            for d in range(2):
-                guarded(lat_sides[d][0], lambda d=d: lat_copy(b, m, d).wait_send())
-                lon_copy(b, m, d).wait_send()
-            return carry
-
-        lax.fori_loop(0, GROUPS, edges_sent, 0)
+    lax.fori_loop(1, steps, returned, 0)
 
 
 def on_device(steps, nlat, nlon, iterate, heating, initial, region, cond_table):

time: 59 us -> 58.8 us (level)
  no operation moved by 1% of the time
where the time goes in v7:
time: 58.8 us; the launch traced here: 58.7 us
  Pallas kernels  57.9 us (98%)
  local copies, waits for them, and re-layouts  0.8 us (1%)
    pallas_call x1, Pallas kernels, on_device(): pl.pallas_call(functools.partial(kernel, steps, nlat, nlon), out_shape=ja...  57.9 us

profile of v7, /device:TPU:1, one launch (start us, length us, event | category | flops | bytes accessed | tf_op | source)
XLA Modules:
  0.0 58.7 jit_solution(4684802577610319833)
XLA Ops:
  0.0 57.9 %shard_map.55 = f32[1024,128]{1,0:T(8,128)S(1)} custom-call(f32[1024,128]{1,0:T(8,128)} %bitcast.7, f32[64,2,8,128]{3,2,1,0:T(8,128)} %bitcast.8, f32[1024,128]{1,0:T(8,128)} %bitcast.9, s32[1024,128]{1,0:T(8,128)} %bitcast.10, f32[1024,128]{1,0:T(8,128)} %bitcast.11, f32[8]{0:T(128)} %table_hbm.1), custom_call_target="tpu_custom_call" | custom-call | tf_op jit(solution)/shard_map/pallas_call | solution.py:706
  57.9 0.8 %copy.7 = f32[1,64,16,128]{3,2,1,0:T(8,128)} copy(f32[1,64,16,128]{3,2,1,0:T(8,128)S(1)} %bitcast.6) | data formatting | bytes 1048576
